TPU v7x, 1024 devices: a whole 8x8x8 slice. The times are simulated.
1024 devices in a mesh: ctx: 128 (over x, y_lo, z), ch: 8 (over y_hi, core).
Axes of the slice: x: 8, y: 8 (y_hi: 4, y_lo: 2; y = y_hi * 2 + y_lo), z: 8, core: 2. Of those that a mesh axis runs over, the one named last changes fastest.
Arguments:
- query_act: bfloat16 [16384, 4096], P('ctx', 'ch'), may hold values from -6 to 6
- key_act: bfloat16 [16384, 4096], P('ctx', 'ch'), may hold values from -6 to 6
- value_act: bfloat16 [16384, 4096], P('ctx', 'ch'), may hold values from -6 to 6
- filters: bfloat16 [256, 128], P('ch'), may hold values from -0.5 to 0.5
- skip_bias: float32 [4096], P('ch'), may hold values from -4 to 4
- out_weight: bfloat16 [4096, 8192], P('ch'), may hold values from -0.09375 to 0.09375
- out_grad: bfloat16 [16384, 8192], P('ctx', 'ch'), may hold values from -6 to 6
Outputs:
- gated: bfloat16 [16384, 4096], P('ctx', 'ch')
- query_grad: bfloat16 [16384, 4096], P('ctx', 'ch')
- key_grad: bfloat16 [16384, 4096], P('ctx', 'ch')
- value_grad: bfloat16 [16384, 4096], P('ctx', 'ch')
- filter_grad: float32 [256, 128], P('ch')
- skip_grad: float32 [4096], P('ch')
All inputs are finite; a program needn't handle non-finite values.
Results may differ from a plain program's by a relative error of at most 0.0075.
Values may be sent and summed in bfloat16 or wider, within the bound.
No kernel may reach another device: no remote copies, remote signals or barrier semaphores. Data moves between devices by JAX's collectives and lax.ppermute only.
A program may use at most 64 MiB of HBM per device.

v0:
```python
import functools

import jax
import jax.numpy as jnp
from jax import lax
from jax.experimental import pallas as pl
from jax.experimental.pallas import tpu as pltpu
from jax.sharding import PartitionSpec as P


BF16 = jnp.bfloat16
F32 = jnp.float32
LANES = 128
Z_SIZE = 8
CORES = 2

VMEM_SPEC = pl.BlockSpec(memory_space=pltpu.VMEM)
SMEM_SPEC = pl.BlockSpec(memory_space=pltpu.SMEM)
NT = (((1,), (1,)), ((), ()))


def dot(a, b):
    return jnp.dot(a, b, preferred_element_type=F32)


def cost(flops, nbytes):
    return pl.CostEstimate(flops=flops, bytes_accessed=nbytes, transcendentals=0)


def group_mask(rows, group, group_size):
    lane = lax.broadcasted_iota(jnp.int32, (rows, LANES), 1)
    return (lane // group_size) == group


def reversal(size):
    row = lax.broadcasted_iota(jnp.int32, (size, size), 0)
    col = lax.broadcasted_iota(jnp.int32, (size, size), 1)
    return (row + col == size - 1).astype(BF16)


def grouped_conv(table_ref, series, group_size):
    tiles = []
    per_tile = LANES // group_size
    for tile in range(series.shape[1] // LANES):
        block = series[:, tile * LANES : (tile + 1) * LANES]
        total = None
        for g in range(per_tile):
            mask = group_mask(block.shape[0], g, group_size)
            part = jnp.where(mask, block, jnp.zeros_like(block))
            term = dot(table_ref[tile * per_tile + g], part)
            total = term if total is None else total + term
        tiles.append(total)
    return jnp.concatenate(tiles, axis=1)


def stage_kernel(filt_ref, weight_hbm, fwd_ref, bwd_ref, weight_ref, sem):
    pieces = sem.shape[0]
    height = weight_hbm.shape[0] // pieces
    copies = []
    for i in range(pieces):
        rows = pl.ds(i * height, height)
        copies.append(
            pltpu.make_async_copy(weight_hbm.at[rows], weight_ref.at[rows], sem.at[i])
        )
        copies[-1].start()
    groups, taps = filt_ref.shape
    filt = filt_ref[...]
    flipped = dot(filt, reversal(taps))
    filt = filt.astype(F32)
    zeros = jnp.zeros((1, taps), F32)
    for g in range(groups):
        for source, out_ref, first in ((flipped, fwd_ref, 1), (filt, bwd_ref, 0)):
            row = jnp.concatenate([source[g : g + 1], zeros], axis=1)
            full = jnp.broadcast_to(row, (taps, 2 * taps))
            out_ref[g] = pltpu.roll(
                full, first, axis=1, stride=1, stride_axis=0
            ).astype(BF16)
    for copy in copies:
        copy.wait()


def forward_kernel(group_size, before_ref, inner_ref, query_ref, skip_ref, fwd_ref,
                   mixed_ref, gated_ref, flipped_ref):
    rows = inner_ref.shape[0]
    inner = inner_ref[...]
    series = jnp.concatenate([before_ref[...], inner], axis=0)
    mixed = grouped_conv(fwd_ref, series, group_size)
    mixed = mixed + skip_ref[...] * inner.astype(F32)
    mixed_ref[...] = mixed
    gated_ref[...] = (query_ref[...].astype(F32) * mixed).astype(BF16)
    flipped_ref[:rows - 16] = jnp.zeros((rows - 16, inner.shape[1]), BF16)
    flipped_ref[rows - 16 :] = dot(reversal(2 * rows), series).astype(BF16)


def product(block, weight_ref, position):
    depth = block.shape[1]
    columns = pl.ds(pl.multiple_of(position * depth, depth), depth)
    return lax.dot_general(block, weight_ref[:, columns], NT, preferred_element_type=F32)


def partial_kernel(start, order_ref, weight_ref, *refs):
    blocks, acc_ref, out_ref = refs[:2], refs[2:-1], refs[-1]
    total = acc_ref[0][...] if acc_ref else None
    for i, block_ref in enumerate(blocks):
        term = product(block_ref[...], weight_ref, order_ref[start + i])
        total = term if total is None else total + term
    out_ref[...] = total


def gradient_kernel(group_size, start, order_ref, weight_ref, first_ref, second_ref, acc_ref,
                    query_ref, mixed_ref, inner_ref, flipped_ref,
                    conv_ref, qgrad_ref, sums_ref):
    rows, width = acc_ref.shape
    mixed_grad = (
        acc_ref[...]
        + product(first_ref[...], weight_ref, order_ref[start])
        + product(second_ref[...], weight_ref, order_ref[start + 1])
    )
    conv = (mixed_grad * query_ref[...].astype(F32)).astype(BF16)
    conv_ref[...] = conv
    qgrad_ref[...] = (mixed_grad * mixed_ref[...]).astype(BF16)
    skip = jnp.sum(conv.astype(F32) * inner_ref[...].astype(F32), axis=0, keepdims=True)
    per_tile = LANES // group_size
    span = 2 * rows
    sub = 16
    row_group = lax.broadcasted_iota(jnp.int32, (per_tile * sub, LANES), 0) // sub
    lane_group = lax.broadcasted_iota(jnp.int32, (per_tile * sub, LANES), 1) // group_size
    own = row_group == lane_group
    for tile in range(width // LANES):
        lanes = slice(tile * LANES, (tile + 1) * LANES)
        total = None
        for a in range(rows // sub):
            part = conv[a * sub : (a + 1) * sub, lanes]
            spread = jnp.concatenate([part] * per_tile, axis=0)
            spread = jnp.where(own, spread, jnp.zeros_like(spread))
            start = rows - sub - a * sub
            term = lax.dot_general(
                spread, flipped_ref[start : start + span, lanes], NT,
                preferred_element_type=F32,
            )
            total = term if total is None else total + term
        for g in range(per_tile):
            skewed = pltpu.roll(
                total[g * sub : (g + 1) * sub], 1, axis=1, stride=1, stride_axis=0
            )
            row = tile * per_tile + g
            sums_ref[row : row + 1] = jnp.sum(skewed[:, rows:], axis=0, keepdims=True)
        row = width // group_size + tile
        sums_ref[row : row + 1] = skip[:, lanes]
    used = width // group_size + width // LANES
    sums_ref[used:] = jnp.zeros((sums_ref.shape[0] - used, LANES), F32)


def backward_kernel(group_size, conv_ref, after_ref, key_ref, value_ref, skip_ref, bwd_ref,
                    kgrad_ref, vgrad_ref):
    conv = conv_ref[...]
    series = jnp.concatenate([conv, after_ref[...]], axis=0)
    grad = grouped_conv(bwd_ref, series, group_size)
    grad = grad + skip_ref[...] * conv.astype(F32)
    kgrad_ref[...] = (grad * value_ref[...].astype(F32)).astype(BF16)
    vgrad_ref[...] = (grad * key_ref[...].astype(F32)).astype(BF16)


def call(kernel, outs, args, flops, specs=None, scratch=(), vmem=24):
    return pl.pallas_call(
        kernel,
        out_shape=[jax.ShapeDtypeStruct(s, d) for s, d in outs],
        in_specs=specs or [VMEM_SPEC] * len(args),
        out_specs=[VMEM_SPEC] * len(outs),
        scratch_shapes=scratch,
        compiler_params=pltpu.CompilerParams(vmem_limit_bytes=vmem << 20),
        cost_estimate=cost(flops, 4 << 20),
    )(*args)


def passed_along(block, axis, distance):
    devices = range(lax.axis_size(axis))
    route = [(i - distance, i) for i in devices if i - distance in devices]
    return lax.ppermute(block, axis, route)


def exchanged(blocks, groups):
    return lax.all_to_all(blocks, "ctx", 0, 0, axis_index_groups=groups, tiled=True)


def spread(block, count):
    return jnp.broadcast_to(block[None], (count,) + block.shape)


def per_device(query_act, key_act, value_act, filters, skip_bias, out_weight, out_grad):
    rows, width = query_act.shape
    groups, taps = filters.shape
    group_size = width // groups
    depth = out_grad.shape[1]
    ch_size = lax.axis_size("ch")
    ctx_size = lax.axis_size("ctx")
    chips = ch_size // CORES

    def ring(block):
        to = lambda c: ((c // CORES + (1 if c % CORES == 0 else -1)) % chips) * CORES + c % CORES
        return lax.ppermute(block, "ch", [(c, to(c)) for c in range(ch_size)])

    def swap(block):
        return lax.ppermute(block, "ch", [(c, c ^ 1) for c in range(ch_size)])

    me = lax.axis_index("ch")
    chip, core = me // CORES, me % CORES
    ahead = jnp.array([0, 0, -1, 1, -1, 1, 2, 2], jnp.int32) * (1 - 2 * core)
    other = jnp.array([0, 1, 0, 1, 1, 0, 0, 1], jnp.int32)
    order = (((chip + ahead) % chips) * CORES + (core ^ other)).astype(jnp.int32)

    skip_row = skip_bias.reshape(1, width)
    inner = (key_act.astype(F32) * value_act.astype(F32)).astype(BF16)

    ring1 = ring(out_grad)
    swap0 = swap(out_grad)
    before = passed_along(inner, "ctx", 1)
    ring2 = ring(swap0)
    fwd, bwd, weight = call(
        stage_kernel,
        [((groups, taps, 2 * taps), BF16)] * 2 + [(out_weight.shape, BF16)],
        (filters, out_weight),
        8 * groups * taps * taps,
        [VMEM_SPEC, pl.BlockSpec(memory_space=pltpu.HBM)],
        [pltpu.SemaphoreType.DMA((8,))],
        40,
    )
    ring3 = ring(ring1)
    swap1 = swap(ring1)
    mixed, gated, flipped = call(
        lambda *refs: forward_kernel(group_size, *refs),
        [((rows, width), F32), ((rows, width), BF16), ((3 * rows - 16, width), BF16)],
        (before, inner, query_act, skip_row, fwd),
        4 * rows * rows * width * 8,
    )
    swap2 = swap(ring2)
    swap3 = swap(ring3)

    acc = ()
    for i, pair in enumerate(((out_grad, swap0), (ring1, swap1), (ring2, swap2))):
        acc = call(
            functools.partial(partial_kernel, 2 * i),
            [((rows, width), F32)],
            (order, weight, *pair, *acc),
            4 * rows * depth * width,
            [SMEM_SPEC] + [VMEM_SPEC] * (3 + len(acc)),
        )
    conv, query_grad, sums = call(
        functools.partial(gradient_kernel, group_size, 6),
        [((rows, width), BF16), ((rows, width), BF16), ((Z_SIZE * 8, LANES), F32)],
        (order, weight, ring3, swap3, *acc, query_act, mixed, inner, flipped),
        8 * rows * depth * width,
        [SMEM_SPEC] + [VMEM_SPEC] * 8,
    )
    planes = ctx_size // Z_SIZE
    along_z = [[p * Z_SIZE + z for z in range(Z_SIZE)] for p in range(planes)]
    across_z = [[p * Z_SIZE + z for p in range(planes)] for z in range(Z_SIZE)]
    sums = jnp.sum(exchanged(sums.reshape(Z_SIZE, 8, LANES), along_z), axis=0)
    after = passed_along(conv, "ctx", -1)
    sums = jnp.sum(exchanged(spread(sums, planes), across_z), axis=0)
    sums = exchanged(spread(sums, Z_SIZE), along_z).reshape(Z_SIZE * 8, LANES)
    key_grad, value_grad = call(
        lambda *refs: backward_kernel(group_size, *refs),
        [((rows, width), BF16)] * 2,
        (conv, after, key_act, value_act, skip_row, bwd),
        4 * rows * rows * width * 8,
    )
    filter_grad = sums[:groups]
    skip_grad = sums[groups : groups + width // LANES].reshape(width)
    return gated, query_grad, key_grad, value_grad, filter_grad, skip_grad


def solution(mesh):
    wide, narrow = P("ctx", "ch"), P("ch", None)

    return jax.shard_map(
        per_device,
        mesh=mesh,
        in_specs=(wide, wide, wide, narrow, P("ch"), narrow, wide),
        out_specs=(wide, wide, wide, wide, narrow, P("ch")),
        check_vma=False,
    )
```

profile of v0, /device:TPU:2, one launch (start us, length us, event | category | flops | bytes accessed | tf_op | source)
XLA Modules:
  0.0 101.6 jit_solution(11234431044189190383)
XLA Ops:
  0.6 0.0 copy-start.6
  0.6 0.0 copy-start.7
  0.7 4.9 %collective-permute-start.1 = (bf16[128,1024]{1,0:T(8,128)(2,1)}, bf16[128,1024]{1,0:T(8,128)(2,1)S(1)}, u32[]{:S(2)}, u32[]{:S(2)}) collective-permute-start(bf16[128,1024]{1,0:T(8,128)(2,1)} %refs_0_.1), channel_id=1, source_target_pairs={{0,2},{1,7},{2,4},{3,1},{4,6},{5,3},{6,0},{7,5},{8,10},{9,15},{10,... | collective-permute-start | bytes 786440 | tf_op jit(solution)/shard_map/ppermute | solution.py:201
  5.6 3.6 %collective-permute-start.4 = (bf16[128,1024]{1,0:T(8,128)(2,1)}, bf16[128,1024]{1,0:T(8,128)(2,1)S(1)}, u32[]{:S(2)}, u32[]{:S(2)}) collective-permute-start(bf16[128,1024]{1,0:T(8,128)(2,1)} %refs_0_.1), channel_id=1, source_target_pairs={{0,1},{1,0},{2,3},{3,2},{4,5},{5,4},{6,7},{7,6},{8,9},{9,8},{10,11... | collective-permute-start | bytes 786440 | tf_op jit(solution)/shard_map/ppermute | solution.py:204
  9.1 3.9 %collective-permute-done.1.refs_0_ = bf16[128,1024]{1,0:T(8,128)(2,1)S(1)} collective-permute-done((bf16[128,1024]{1,0:T(8,128)(2,1)}, bf16[128,1024]{1,0:T(8,128)(2,1)S(1)}, u32[]{:S(2)}, u32[]{:S(2)}) %collective-permute-start.1) | collective-permute-done | bytes 262176 | tf_op jit(solution)/shard_map/ppermute | solution.py:201
  13.0 4.9 %collective-permute-start.2 = (bf16[128,1024]{1,0:T(8,128)(2,1)S(1)}, bf16[128,1024]{1,0:T(8,128)(2,1)S(1)}, u32[]{:S(2)}, u32[]{:S(2)}) collective-permute-start(bf16[128,1024]{1,0:T(8,128)(2,1)S(1)} %collective-permute-done.1.refs_0_), channel_id=1, source_target_pairs={{0,2},{1,7},{2,4},{3,1},{4,6},{5,3},{6,0},{7,5},{8,10},{9,15},{10,... | collective-permute-start | bytes 786440 | tf_op jit(solution)/shard_map/ppermute | solution.py:201
  18.0 6.4 %collective-permute-start.5 = (bf16[128,1024]{1,0:T(8,128)(2,1)S(1)}, bf16[128,1024]{1,0:T(8,128)(2,1)}, u32[]{:S(2)}, u32[]{:S(2)}) collective-permute-start(bf16[128,1024]{1,0:T(8,128)(2,1)S(1)} %collective-permute-done.4.refs_1_), channel_id=1, source_target_pairs={{0,2},{1,7},{2,4},{3,1},{4,6},{5,3},{6,0},{7,5},{8,10},{9,15},{10,... | collective-permute-start | bytes 786440 | tf_op jit(solution)/shard_map/ppermute | solution.py:201
  24.4 1.0 multiply_convert_fusion.refs_1_.inner_ref
  25.4 5.2 %collective-permute-start = (bf16[128,512]{1,0:T(8,128)(2,1)S(1)}, bf16[128,512]{1,0:T(8,128)(2,1)S(1)}, u32[]{:S(2)}, u32[]{:S(2)}) collective-permute-start(bf16[128,512]{1,0:T(8,128)(2,1)S(1)} %multiply_convert_fusion.refs_1_.inner_ref), channel_id=1, source_target_pairs={{0,8},{8,16},{16,24},{24,32},{32,40},{40,48},{48,56},{56,64},{64,7... | collective-permute-start | bytes 393224 | tf_op jit(solution)/shard_map/ppermute | solution.py:179
  30.6 0.7 copy-done.4
  31.3 4.3 %shard_map.136 = (bf16[32,128,256]{2,1,0:T(8,128)(2,1)S(1)}, bf16[32,128,256]{2,1,0:T(8,128)(2,1)S(1)}, bf16[512,8192]{1,0:T(8,128)(2,1)S(1)}) custom-call(bf16[32,128]{1,0:T(8,128)(2,1)S(1)} %copy-done.4, bf16[512,8192]{1,0:T(8,128)(2,1)} %weight_hbm.1), custom_call_target="tpu_custom_call" | custom-call | flops 4194304 | bytes 4194304 | tf_op jit(solution)/shard_map/pallas_call | solution.py:165
  35.5 1.9 %collective-permute-start.7 = (bf16[128,1024]{1,0:T(8,128)(2,1)S(1)}, bf16[128,1024]{1,0:T(8,128)(2,1)S(1)}, u32[]{:S(2)}, u32[]{:S(2)}) collective-permute-start(bf16[128,1024]{1,0:T(8,128)(2,1)S(1)} %collective-permute-done.1.refs_0_), channel_id=1, source_target_pairs={{0,1},{1,0},{2,3},{3,2},{4,5},{5,4},{6,7},{7,6},{8,9},{9,8},{10,11... | collective-permute-start | bytes 786440 | tf_op jit(solution)/shard_map/ppermute | solution.py:204
  37.5 2.4 %collective-permute-start.3 = (bf16[128,1024]{1,0:T(8,128)(2,1)S(1)}, bf16[128,1024]{1,0:T(8,128)(2,1)S(1)}, u32[]{:S(2)}, u32[]{:S(2)}) collective-permute-start(bf16[128,1024]{1,0:T(8,128)(2,1)S(1)} %collective-permute-done.2.first_ref), channel_id=1, source_target_pairs={{0,1},{1,0},{2,3},{3,2},{4,5},{5,4},{6,7},{7,6},{8,9},{9,8},{10,11... | collective-permute-start | bytes 786440 | tf_op jit(solution)/shard_map/ppermute | solution.py:204
  39.9 1.9 %collective-permute-start.6 = (bf16[128,1024]{1,0:T(8,128)(2,1)}, bf16[128,1024]{1,0:T(8,128)(2,1)S(1)}, u32[]{:S(2)}, u32[]{:S(2)}) collective-permute-start(bf16[128,1024]{1,0:T(8,128)(2,1)} %collective-permute-done.5.refs_0_), channel_id=1, source_target_pairs={{0,1},{1,0},{2,3},{3,2},{4,5},{5,4},{6,7},{7,6},{8,9},{9,8},{10,11... | collective-permute-start | bytes 786440 | tf_op jit(solution)/shard_map/ppermute | solution.py:204
  41.9 5.2 %collective-permute-done.refs_0_ = bf16[128,512]{1,0:T(8,128)(2,1)S(1)} collective-permute-done((bf16[128,512]{1,0:T(8,128)(2,1)S(1)}, bf16[128,512]{1,0:T(8,128)(2,1)S(1)}, u32[]{:S(2)}, u32[]{:S(2)}) %collective-permute-start) | collective-permute-done | bytes 131104 | tf_op jit(solution)/shard_map/ppermute | solution.py:179
  47.1 1.4 %shard_map.137 = (f32[128,512]{1,0:T(8,128)S(1)}, bf16[128,512]{1,0:T(8,128)(2,1)}, bf16[368,512]{1,0:T(8,128)(2,1)S(1)}) custom-call(bf16[128,512]{1,0:T(8,128)(2,1)S(1)} %collective-permute-done.refs_0_, bf16[128,512]{1,0:T(8,128)(2,1)S(1)} %multiply_convert_fusion.refs_1_.inner_ref, bf16[128,512]{1,0:T(8,128)(2,1)S(1)} %copy-done, f32[1,512]{1,0:T(1,128)S(1)} %bitcast.8, ...), custom_call_target="tpu_custom_call" | custom-call | flops 268435456 | bytes 4194304 | tf_op jit(solution)/shard_map/pallas_call | solution.py:165
  48.5 1.4 %shard_map.138.refs_2_ = f32[128,512]{1,0:T(8,128)S(1)} custom-call(s32[8]{0:T(128)S(1)} %fusion.1.order_ref, bf16[512,8192]{1,0:T(8,128)(2,1)S(1)} %get-tuple-element.19.weight_ref, bf16[128,1024]{1,0:T(8,128)(2,1)S(1)} %copy-done.3, bf16[128,1024]{1,0:T(8,128)(2,1)S(1)} %collective-permute-done.4.refs_1_), custom_call_target="tpu_custom_call" | custom-call | flops 268435456 | bytes 4194304 | tf_op jit(solution)/shard_map/pallas_call | solution.py:165
  49.9 1.4 %shard_map.139.refs_2_ = f32[128,512]{1,0:T(8,128)S(1)} custom-call(s32[8]{0:T(128)S(1)} %fusion.1.order_ref, bf16[512,8192]{1,0:T(8,128)(2,1)S(1)} %get-tuple-element.19.weight_ref, bf16[128,1024]{1,0:T(8,128)(2,1)S(1)} %collective-permute-done.1.refs_0_, bf16[128,1024]{1,0:T(8,128)(2,1)S(1)} %collective-permute-done.7.refs_1_, ...), custom_call_target="tpu_custom_call" | custom-call | flops 268435456 | bytes 4194304 | tf_op jit(solution)/shard_map/pallas_call | solution.py:165
  51.3 0.0 copy-start.1
  51.3 1.8 %shard_map.140.acc_ref = f32[128,512]{1,0:T(8,128)S(1)} custom-call(s32[8]{0:T(128)S(1)} %fusion.1.order_ref, bf16[512,8192]{1,0:T(8,128)(2,1)S(1)} %get-tuple-element.19.weight_ref, bf16[128,1024]{1,0:T(8,128)(2,1)} %collective-permute-done.5.refs_0_, bf16[128,1024]{1,0:T(8,128)(2,1)S(1)} %collective-permute-done.6.refs_1_, f32[128,512]{1,0:T(8,128)S(1)} %shard_map.139.refs_2_), custom_call_target="tpu_custom_call" | custom-call | flops 268435456 | bytes 4194304 | tf_op jit(solution)/shard_map/pallas_call | solution.py:165
  53.2 2.2 %shard_map.141 = (bf16[128,512]{1,0:T(8,128)(2,1)S(1)}, bf16[128,512]{1,0:T(8,128)(2,1)}, f32[64,128]{1,0:T(8,128)S(1)}) custom-call(s32[8]{0:T(128)S(1)} %fusion.1.order_ref, bf16[512,8192]{1,0:T(8,128)(2,1)S(1)} %get-tuple-element.19.weight_ref, bf16[128,1024]{1,0:T(8,128)(2,1)S(1)} %collective-permute-done.2.first_ref, ...), custom_call_target="tpu_custom_call" | custom-call | flops 536870912 | bytes 4194304 | tf_op jit(solution)/shard_map/pallas_call | solution.py:165
  55.4 17.6 %all_to_all.15 = f32[8,8,128]{2,1,0:T(8,128)S(1)} all-to-all(f32[8,8,128]{2,1,0:T(8,128)S(1)} %bitcast.7), channel_id=1, replica_groups={{0,8,16,24,32,40,48,56},{64,72,80,88,96,104,112,120},{128,136,144,152,1..., dimensions={0} | all-to-all | bytes 65536 | tf_op jit(solution)/shard_map/all_to_all | solution.py:183
  73.0 0.6 broadcast_in_dim.4
  73.6 7.3 %all-to-all-start.1 = ((f32[16,8,128]{2,1,0:T(8,128)}), f32[16,8,128]{2,1,0:T(8,128)S(1)}, u32[]{:S(2)}, u32[]{:S(2)}) async-start(f32[16,8,128]{2,1,0:T(8,128)} %broadcast_in_dim.4), calls=%async_computation.1 | async-start | bytes 131072 | tf_op jit(solution)/shard_map/all_to_all | solution.py:183
  80.9 3.2 %collective-permute-start.8 = (bf16[128,512]{1,0:T(8,128)(2,1)S(1)}, bf16[128,512]{1,0:T(8,128)(2,1)S(1)}, u32[]{:S(2)}, u32[]{:S(2)}) collective-permute-start(bf16[128,512]{1,0:T(8,128)(2,1)S(1)} %get-tuple-element.23.refs_0_), channel_id=1, source_target_pairs={{8,0},{16,8},{24,16},{32,24},{40,32},{48,40},{56,48},{64,56},{72,6... | collective-permute-start | bytes 393224 | tf_op jit(solution)/shard_map/ppermute | solution.py:179
  84.1 4.4 %all-to-all-done.1 = f32[16,8,128]{2,1,0:T(8,128)S(1)} async-done(((f32[16,8,128]{2,1,0:T(8,128)}), f32[16,8,128]{2,1,0:T(8,128)S(1)}, u32[]{:S(2)}, u32[]{:S(2)}) %all-to-all-start.1) | async-done | bytes 65568 | tf_op jit(solution)/shard_map/all_to_all | solution.py:183
  88.5 0.6 broadcast_in_dim.5
  89.2 3.3 %all-to-all-start.2 = ((f32[8,8,128]{2,1,0:T(8,128)}), f32[8,8,128]{2,1,0:T(8,128)S(1)}, u32[]{:S(2)}, u32[]{:S(2)}) async-start(f32[8,8,128]{2,1,0:T(8,128)} %broadcast_in_dim.5), calls=%async_computation.2 | async-start | bytes 65536 | tf_op jit(solution)/shard_map/all_to_all | solution.py:183
  92.5 1.4 %shard_map.142 = (bf16[128,512]{1,0:T(8,128)(2,1)}, bf16[128,512]{1,0:T(8,128)(2,1)}) custom-call(bf16[128,512]{1,0:T(8,128)(2,1)S(1)} %get-tuple-element.23.refs_0_, bf16[128,512]{1,0:T(8,128)(2,1)S(1)} %collective-permute-done.8.refs_1_, bf16[128,512]{1,0:T(8,128)(2,1)S(1)} %copy-done.2, bf16[128,512]{1,0:T(8,128)(2,1)S(1)} %copy-done.1, ...), custom_call_target="tpu_custom_call" | custom-call | flops 268435456 | bytes 4194304 | tf_op jit(solution)/shard_map/pallas_call | solution.py:165
  93.9 6.5 %all-to-all-done.2 = f32[8,8,128]{2,1,0:T(8,128)S(1)} async-done(((f32[8,8,128]{2,1,0:T(8,128)}), f32[8,8,128]{2,1,0:T(8,128)S(1)}, u32[]{:S(2)}, u32[]{:S(2)}) %all-to-all-start.2) | async-done | bytes 32800 | tf_op jit(solution)/shard_map/all_to_all | solution.py:183
  100.4 0.6 slice_bitcast_fusion.1
  101.0 0.6 slice_bitcast_fusion
  (22 shorter events, 0.1 us)
Async XLA Ops:
  0.6 41.2 %copy-start.6 = (s32[8]{0:T(128)S(1)}, s32[8]{0:T(128)}, u32[]{:S(2)}) copy-start(s32[8]{0:T(128)} %constant.51.clone) | copy-start | bytes 100
  0.6 41.2 %copy-start.7 = (s32[8]{0:T(128)S(1)}, s32[8]{0:T(128)}, u32[]{:S(2)}) copy-start(s32[8]{0:T(128)} %constant.50.clone) | copy-start | bytes 100
  0.7 47.8 %copy-start.3 = (bf16[128,1024]{1,0:T(8,128)(2,1)S(1)}, bf16[128,1024]{1,0:T(8,128)(2,1)}, u32[]{:S(2)}) copy-start(bf16[128,1024]{1,0:T(8,128)(2,1)} %refs_0_.1) | copy-start | bytes 786436
  0.7 46.4 %copy-start = (bf16[128,512]{1,0:T(8,128)(2,1)S(1)}, bf16[128,512]{1,0:T(8,128)(2,1)}, u32[]{:S(2)}) copy-start(bf16[128,512]{1,0:T(8,128)(2,1)} %query_ref.1) | copy-start | bytes 393220
  0.7 46.4 %copy-start.5 = (f32[512]{0:T(512)S(1)}, f32[512]{0:T(512)}, u32[]{:S(2)}) copy-start(f32[512]{0:T(512)} %param.13) | copy-start | bytes 6148
  0.7 12.3 %collective-permute-start.1 = (bf16[128,1024]{1,0:T(8,128)(2,1)}, bf16[128,1024]{1,0:T(8,128)(2,1)S(1)}, u32[]{:S(2)}, u32[]{:S(2)}) collective-permute-start(bf16[128,1024]{1,0:T(8,128)(2,1)} %refs_0_.1), channel_id=1, source_target_pairs={{0,2},{1,7},{2,4},{3,1},{4,6},{5,3},{6,0},{7,5},{8,10},{9,15},{10,... | collective-permute-start | bytes 786440 | tf_op jit(solution)/shard_map/ppermute | solution.py:201
  5.6 12.4 %collective-permute-start.4 = (bf16[128,1024]{1,0:T(8,128)(2,1)}, bf16[128,1024]{1,0:T(8,128)(2,1)S(1)}, u32[]{:S(2)}, u32[]{:S(2)}) collective-permute-start(bf16[128,1024]{1,0:T(8,128)(2,1)} %refs_0_.1), channel_id=1, source_target_pairs={{0,1},{1,0},{2,3},{3,2},{4,5},{5,4},{6,7},{7,6},{8,9},{9,8},{10,11... | collective-permute-start | bytes 786440 | tf_op jit(solution)/shard_map/ppermute | solution.py:204
  13.0 24.4 %collective-permute-start.2 = (bf16[128,1024]{1,0:T(8,128)(2,1)S(1)}, bf16[128,1024]{1,0:T(8,128)(2,1)S(1)}, u32[]{:S(2)}, u32[]{:S(2)}) collective-permute-start(bf16[128,1024]{1,0:T(8,128)(2,1)S(1)} %collective-permute-done.1.refs_0_), channel_id=1, source_target_pairs={{0,2},{1,7},{2,4},{3,1},{4,6},{5,3},{6,0},{7,5},{8,10},{9,15},{10,... | collective-permute-start | bytes 786440 | tf_op jit(solution)/shard_map/ppermute | solution.py:201
  18.0 22.0 %collective-permute-start.5 = (bf16[128,1024]{1,0:T(8,128)(2,1)S(1)}, bf16[128,1024]{1,0:T(8,128)(2,1)}, u32[]{:S(2)}, u32[]{:S(2)}) collective-permute-start(bf16[128,1024]{1,0:T(8,128)(2,1)S(1)} %collective-permute-done.4.refs_1_), channel_id=1, source_target_pairs={{0,2},{1,7},{2,4},{3,1},{4,6},{5,3},{6,0},{7,5},{8,10},{9,15},{10,... | collective-permute-start | bytes 786440 | tf_op jit(solution)/shard_map/ppermute | solution.py:201
  25.4 21.7 %collective-permute-start = (bf16[128,512]{1,0:T(8,128)(2,1)S(1)}, bf16[128,512]{1,0:T(8,128)(2,1)S(1)}, u32[]{:S(2)}, u32[]{:S(2)}) collective-permute-start(bf16[128,512]{1,0:T(8,128)(2,1)S(1)} %multiply_convert_fusion.refs_1_.inner_ref), channel_id=1, source_target_pairs={{0,8},{8,16},{16,24},{24,32},{32,40},{40,48},{48,56},{56,64},{64,7... | collective-permute-start | bytes 393224 | tf_op jit(solution)/shard_map/ppermute | solution.py:179
  30.6 0.7 copy-start.4
  35.5 14.3 %collective-permute-start.7 = (bf16[128,1024]{1,0:T(8,128)(2,1)S(1)}, bf16[128,1024]{1,0:T(8,128)(2,1)S(1)}, u32[]{:S(2)}, u32[]{:S(2)}) collective-permute-start(bf16[128,1024]{1,0:T(8,128)(2,1)S(1)} %collective-permute-done.1.refs_0_), channel_id=1, source_target_pairs={{0,1},{1,0},{2,3},{3,2},{4,5},{5,4},{6,7},{7,6},{8,9},{9,8},{10,11... | collective-permute-start | bytes 786440 | tf_op jit(solution)/shard_map/ppermute | solution.py:204
  37.5 15.7 %collective-permute-start.3 = (bf16[128,1024]{1,0:T(8,128)(2,1)S(1)}, bf16[128,1024]{1,0:T(8,128)(2,1)S(1)}, u32[]{:S(2)}, u32[]{:S(2)}) collective-permute-start(bf16[128,1024]{1,0:T(8,128)(2,1)S(1)} %collective-permute-done.2.first_ref), channel_id=1, source_target_pairs={{0,1},{1,0},{2,3},{3,2},{4,5},{5,4},{6,7},{7,6},{8,9},{9,8},{10,11... | collective-permute-start | bytes 786440 | tf_op jit(solution)/shard_map/ppermute | solution.py:204
  39.9 11.4 %collective-permute-start.6 = (bf16[128,1024]{1,0:T(8,128)(2,1)}, bf16[128,1024]{1,0:T(8,128)(2,1)S(1)}, u32[]{:S(2)}, u32[]{:S(2)}) collective-permute-start(bf16[128,1024]{1,0:T(8,128)(2,1)} %collective-permute-done.5.refs_0_), channel_id=1, source_target_pairs={{0,1},{1,0},{2,3},{3,2},{4,5},{5,4},{6,7},{7,6},{8,9},{9,8},{10,11... | collective-permute-start | bytes 786440 | tf_op jit(solution)/shard_map/ppermute | solution.py:204
  51.3 41.2 %copy-start.1 = (bf16[128,512]{1,0:T(8,128)(2,1)S(1)}, bf16[128,512]{1,0:T(8,128)(2,1)}, u32[]{:S(2)}) copy-start(bf16[128,512]{1,0:T(8,128)(2,1)} %refs_3_.1) | copy-start | bytes 393220
  51.3 41.2 %copy-start.2 = (bf16[128,512]{1,0:T(8,128)(2,1)S(1)}, bf16[128,512]{1,0:T(8,128)(2,1)}, u32[]{:S(2)}) copy-start(bf16[128,512]{1,0:T(8,128)(2,1)} %refs_2_.3) | copy-start | bytes 393220
  73.6 14.9 %all-to-all-start.1 = ((f32[16,8,128]{2,1,0:T(8,128)}), f32[16,8,128]{2,1,0:T(8,128)S(1)}, u32[]{:S(2)}, u32[]{:S(2)}) async-start(f32[16,8,128]{2,1,0:T(8,128)} %broadcast_in_dim.4), calls=%async_computation.1 | async-start | bytes 131072 | tf_op jit(solution)/shard_map/all_to_all | solution.py:183
  80.9 11.6 %collective-permute-start.8 = (bf16[128,512]{1,0:T(8,128)(2,1)S(1)}, bf16[128,512]{1,0:T(8,128)(2,1)S(1)}, u32[]{:S(2)}, u32[]{:S(2)}) collective-permute-start(bf16[128,512]{1,0:T(8,128)(2,1)S(1)} %get-tuple-element.23.refs_0_), channel_id=1, source_target_pairs={{8,0},{16,8},{24,16},{32,24},{40,32},{48,40},{56,48},{64,56},{72,6... | collective-permute-start | bytes 393224 | tf_op jit(solution)/shard_map/ppermute | solution.py:179
  89.2 11.3 %all-to-all-start.2 = ((f32[8,8,128]{2,1,0:T(8,128)}), f32[8,8,128]{2,1,0:T(8,128)S(1)}, u32[]{:S(2)}, u32[]{:S(2)}) async-start(f32[8,8,128]{2,1,0:T(8,128)} %broadcast_in_dim.5), calls=%async_computation.2 | async-start | bytes 65536 | tf_op jit(solution)/shard_map/all_to_all | solution.py:183
where the time goes:
time: 102 us
  starting transfers between devices  45 us (44%)
  waiting for transfers between devices  20.1 us (20%)
  blocking collectives  17.6 us (17%)
  Pallas kernels  13.8 us (14%)
  local copies, waits for them, and re-layouts  3.17 us (3%)
  other arithmetic  1.05 us (1%)
    all_to_all x1, blocking collectives, exchanged(): lax.all_to_all(blocks, 'ctx', 0, 0, axis_index_groups=groups, tiled=True)  17.6 us
    ppermute x3, starting transfers between devices, ring(): return lax.ppermute(block, 'ch', [(c, to(c)) for c in range(ch_size)])  16.1 us
    pallas_call x7, Pallas kernels, call(): pl.pallas_call(kernel, out_shape=[jax.ShapeDtypeStruct(s, d) for s, d in...  13.8 us
    all_to_all x2, waiting for transfers between devices, exchanged(): lax.all_to_all(blocks, 'ctx', 0, 0, axis_index_groups=groups, tiled=True)  10.9 us
    all_to_all x2, starting transfers between devices, exchanged(): lax.all_to_all(blocks, 'ctx', 0, 0, axis_index_groups=groups, tiled=True)  10.6 us
    ppermute x4, starting transfers between devices, swap(): return lax.ppermute(block, 'ch', [(c, c ^ 1) for c in range(ch_size)])  9.83 us
    ppermute x2, starting transfers between devices, passed_along(): return lax.ppermute(block, axis, route)  8.37 us
    ppermute x2, waiting for transfers between devices, passed_along(): return lax.ppermute(block, axis, route)  5.23 us
  transfers between devices with their start and end apart: 11, of which 4 were waited for; matrix products, arithmetic and copies ran while one was open for 2% of the time, Pallas kernels for 11%

commit v1 on v0

v1 whole, which is shorter than its diff:
```python
import functools

import jax
import jax.numpy as jnp
from jax import lax
from jax.experimental import pallas as pl
from jax.experimental.pallas import tpu as pltpu
from jax.sharding import PartitionSpec as P


BF16 = jnp.bfloat16
F32 = jnp.float32
LANES = 128
Z_SIZE = 8
CORES = 2
SUM_ROWS = 40
VMEM_MIB = 44
PAIR_DISTANCE = (0, -1, 1, 2)
SWAPPED_PAIR = 2

VMEM_SPEC = pl.BlockSpec(memory_space=pltpu.VMEM)
NT = (((1,), (1,)), ((), ()))


def dot(a, b):
    return jnp.dot(a, b, preferred_element_type=F32)


def cost(flops, nbytes):
    return pl.CostEstimate(flops=flops, bytes_accessed=nbytes, transcendentals=0)


def group_mask(rows, group, group_size):
    lane = lax.broadcasted_iota(jnp.int32, (rows, LANES), 1)
    return (lane // group_size) == group


def reversal(size):
    row = lax.broadcasted_iota(jnp.int32, (size, size), 0)
    col = lax.broadcasted_iota(jnp.int32, (size, size), 1)
    return (row + col == size - 1).astype(BF16)


def grouped_conv(table_ref, series, group_size):
    tiles = []
    per_tile = LANES // group_size
    for tile in range(series.shape[1] // LANES):
        block = series[:, tile * LANES : (tile + 1) * LANES]
        total = None
        for g in range(per_tile):
            mask = group_mask(block.shape[0], g, group_size)
            part = jnp.where(mask, block, jnp.zeros_like(block))
            term = dot(table_ref[tile * per_tile + g], part)
            total = term if total is None else total + term
        tiles.append(total)
    return jnp.concatenate(tiles, axis=1)


def positions(pair):
    size = lax.axis_size("ch")
    me = lax.axis_index("ch")
    chips = size // CORES
    chip, core = me // CORES, me % CORES
    step = 1 - 2 * core
    owner = (chip + PAIR_DISTANCE[pair] * step + chips) % chips
    first = 1 - core if pair == SWAPPED_PAIR else core
    return [owner * CORES + first, owner * CORES + 1 - first]


def fetched(weight_hbm, pair_ref, sem, pair):
    depth = pair_ref.shape[2]
    copies = []
    for i, position in enumerate(positions(pair)):
        columns = pl.ds(pl.multiple_of(position * depth, depth), depth)
        copies.append(
            pltpu.make_async_copy(weight_hbm.at[:, columns], pair_ref.at[i], sem.at[i])
        )
        copies[-1].start()
    return copies


def finished(copies):
    for copy in copies:
        copy.wait()


def stage_kernel(filt_ref, weight_hbm, fwd_ref, bwd_ref, pair_ref, sem):
    copies = fetched(weight_hbm, pair_ref, sem, 0)
    groups, taps = filt_ref.shape
    filt = filt_ref[...]
    flipped = dot(filt, reversal(taps))
    filt = filt.astype(F32)
    zeros = jnp.zeros((1, taps), F32)
    for g in range(groups):
        for source, out_ref, first in ((flipped, fwd_ref, 1), (filt, bwd_ref, 0)):
            row = jnp.concatenate([source[g : g + 1], zeros], axis=1)
            full = jnp.broadcast_to(row, (taps, 2 * taps))
            out_ref[g] = pltpu.roll(
                full, first, axis=1, stride=1, stride_axis=0
            ).astype(BF16)
    finished(copies)


def forward_kernel(group_size, before_ref, inner_ref, query_ref, skip_ref, fwd_ref,
                   ring1_ref, ring2_ref, weight_hbm,
                   mixed_ref, gated_ref, flipped_ref, packed_ref, pair_ref, sem):
    copies = fetched(weight_hbm, pair_ref, sem, 2)
    packed_ref[0] = ring1_ref[...]
    packed_ref[1] = ring2_ref[...]
    rows = inner_ref.shape[0]
    inner = inner_ref[...]
    series = jnp.concatenate([before_ref[...], inner], axis=0)
    mixed = grouped_conv(fwd_ref, series, group_size)
    mixed = mixed + skip_ref[...] * inner.astype(F32)
    mixed_ref[...] = mixed
    gated_ref[...] = (query_ref[...].astype(F32) * mixed).astype(BF16)
    flipped_ref[:rows - 16] = jnp.zeros((rows - 16, inner.shape[1]), BF16)
    flipped_ref[rows - 16 :] = dot(reversal(2 * rows), series).astype(BF16)
    finished(copies)


def products(blocks, pair_ref):
    total = None
    for i, block in enumerate(blocks):
        term = lax.dot_general(block, pair_ref[i], NT, preferred_element_type=F32)
        total = term if total is None else total + term
    return total


def first_product_kernel(own_ref, swap_ref, pair_ref, weight_hbm, out_ref, next_ref, sem):
    copies = fetched(weight_hbm, next_ref, sem, 1)
    out_ref[...] = products((own_ref[...], swap_ref[...]), pair_ref)
    finished(copies)


def second_product_kernel(ring1_ref, ring2_ref, pair_ref, acc_ref, weight_hbm,
                          out_ref, next_ref, sem):
    copies = fetched(weight_hbm, next_ref, sem, 3)
    out_ref[...] = acc_ref[...] + products((ring1_ref[...], ring2_ref[...]), pair_ref)
    finished(copies)


def third_product_kernel(swaps_ref, pair_ref, acc_ref, out_ref):
    out_ref[...] = acc_ref[...] + products((swaps_ref[0], swaps_ref[1]), pair_ref)


def gradient_kernel(group_size, pair_ref, first_ref, second_ref, acc_ref,
                    query_ref, mixed_ref, inner_ref, flipped_ref,
                    conv_ref, qgrad_ref, sums_ref):
    rows, width = acc_ref.shape
    mixed_grad = acc_ref[...] + products((first_ref[...], second_ref[...]), pair_ref)
    conv = (mixed_grad * query_ref[...].astype(F32)).astype(BF16)
    conv_ref[...] = conv
    qgrad_ref[...] = (mixed_grad * mixed_ref[...]).astype(BF16)
    skip = jnp.sum(conv.astype(F32) * inner_ref[...].astype(F32), axis=0, keepdims=True)
    per_tile = LANES // group_size
    span = 2 * rows
    sub = 16
    row_group = lax.broadcasted_iota(jnp.int32, (per_tile * sub, LANES), 0) // sub
    lane_group = lax.broadcasted_iota(jnp.int32, (per_tile * sub, LANES), 1) // group_size
    own = row_group == lane_group
    found = []
    for tile in range(width // LANES):
        lanes = slice(tile * LANES, (tile + 1) * LANES)
        total = None
        for a in range(rows // sub):
            part = conv[a * sub : (a + 1) * sub, lanes]
            spread = jnp.concatenate([part] * per_tile, axis=0)
            spread = jnp.where(own, spread, jnp.zeros_like(spread))
            start = rows - sub - a * sub
            term = lax.dot_general(
                spread, flipped_ref[start : start + span, lanes], NT,
                preferred_element_type=F32,
            )
            total = term if total is None else total + term
        for g in range(per_tile):
            skewed = pltpu.roll(
                total[g * sub : (g + 1) * sub], 1, axis=1, stride=1, stride_axis=0
            )
            found.append(jnp.sum(skewed[:, rows:], axis=0, keepdims=True))
    found += [skip[:, i * LANES : (i + 1) * LANES] for i in range(width // LANES)]
    found.append(jnp.zeros((sums_ref.shape[1] - len(found), LANES), F32))
    sums = jnp.concatenate(found, axis=0)
    for i in range(sums_ref.shape[0]):
        sums_ref[i] = sums


def fold_kernel(got_ref, out_ref):
    total = jnp.sum(got_ref[...], axis=0)
    for i in range(out_ref.shape[0]):
        out_ref[i] = total


def finish_kernel(got_ref, filter_ref, skip_ref):
    total = jnp.sum(got_ref[...], axis=0)
    groups = filter_ref.shape[0]
    filter_ref[...] = total[:groups]
    for i in range(skip_ref.shape[1] // LANES):
        skip_ref[:, i * LANES : (i + 1) * LANES] = total[groups + i : groups + i + 1]


def backward_kernel(group_size, conv_ref, after_ref, key_ref, value_ref, skip_ref, bwd_ref,
                    kgrad_ref, vgrad_ref):
    conv = conv_ref[...]
    series = jnp.concatenate([conv, after_ref[...]], axis=0)
    grad = grouped_conv(bwd_ref, series, group_size)
    grad = grad + skip_ref[...] * conv.astype(F32)
    kgrad_ref[...] = (grad * value_ref[...].astype(F32)).astype(BF16)
    vgrad_ref[...] = (grad * key_ref[...].astype(F32)).astype(BF16)


def call(kernel, outs, args, flops, specs=None, scratch=(), vmem=24):
    return pl.pallas_call(
        kernel,
        out_shape=[jax.ShapeDtypeStruct(s, d) for s, d in outs],
        in_specs=specs or [VMEM_SPEC] * len(args),
        out_specs=[VMEM_SPEC] * len(outs),
        scratch_shapes=scratch,
        compiler_params=pltpu.CompilerParams(vmem_limit_bytes=vmem << 20),
        cost_estimate=cost(flops, 4 << 20),
    )(*args)


def passed_along(block, axis, distance):
    devices = range(lax.axis_size(axis))
    route = [(i - distance, i) for i in devices if i - distance in devices]
    return lax.ppermute(block, axis, route)


def exchanged(blocks, groups):
    return lax.all_to_all(blocks, "ctx", 0, 0, axis_index_groups=groups, tiled=True)


def per_device(query_act, key_act, value_act, filters, skip_bias, out_weight, out_grad):
    rows, width = query_act.shape
    groups, taps = filters.shape
    group_size = width // groups
    depth = out_grad.shape[1]
    ch_size = lax.axis_size("ch")
    ctx_size = lax.axis_size("ctx")
    chips = ch_size // CORES

    def ring(block):
        to = lambda c: ((c // CORES + (1 if c % CORES == 0 else -1)) % chips) * CORES + c % CORES
        return lax.ppermute(block, "ch", [(c, to(c)) for c in range(ch_size)])

    def swap(block):
        return lax.ppermute(block, "ch", [(c, c ^ 1) for c in range(ch_size)])

    skip_row = skip_bias.reshape(1, width)
    inner = (key_act.astype(F32) * value_act.astype(F32)).astype(BF16)

    hbm = pl.BlockSpec(memory_space=pltpu.HBM)
    pair = ((2, width, depth), BF16)
    wide = (rows, width)
    sem = [pltpu.SemaphoreType.DMA((2,))]

    ring1 = ring(out_grad)
    swap0 = swap(out_grad)
    before = passed_along(inner, "ctx", 1)
    ring2 = ring(swap0)
    fwd, bwd, pair0 = call(
        stage_kernel,
        [((groups, taps, 2 * taps), BF16)] * 2 + [pair],
        (filters, out_weight),
        8 * groups * taps * taps,
        [VMEM_SPEC, hbm],
        sem,
        VMEM_MIB,
    )
    acc, pair1 = call(
        first_product_kernel,
        [(wide, F32), pair],
        (out_grad, swap0, pair0, out_weight),
        4 * rows * depth * width,
        [VMEM_SPEC] * 3 + [hbm],
        sem,
        VMEM_MIB,
    )
    ring3 = ring(ring1)
    mixed, gated, flipped, packed, pair2 = call(
        functools.partial(forward_kernel, group_size),
        [(wide, F32), (wide, BF16), ((3 * rows - 16, width), BF16), ((2, rows, depth), BF16), pair],
        (before, inner, query_act, skip_row, fwd, ring1, ring2, out_weight),
        4 * rows * rows * width * 8,
        [VMEM_SPEC] * 7 + [hbm],
        sem,
        VMEM_MIB,
    )
    swap12 = swap(packed)
    acc, pair3 = call(
        second_product_kernel,
        [(wide, F32), pair],
        (ring1, ring2, pair1, acc, out_weight),
        4 * rows * depth * width,
        [VMEM_SPEC] * 4 + [hbm],
        sem,
        VMEM_MIB,
    )
    swap3 = swap(ring3)
    acc = call(
        third_product_kernel, [(wide, F32)], (swap12, pair2, acc), 4 * rows * depth * width
    )[0]
    planes = ctx_size // Z_SIZE
    conv, query_grad, sums = call(
        functools.partial(gradient_kernel, group_size),
        [(wide, BF16), (wide, BF16), ((Z_SIZE, SUM_ROWS, LANES), F32)],
        (pair3, ring3, swap3, acc, query_act, mixed, inner, flipped),
        8 * rows * depth * width,
    )
    along_z = [[p * Z_SIZE + z for z in range(Z_SIZE)] for p in range(planes)]
    across_z = [[p * Z_SIZE + z for p in range(planes)] for z in range(Z_SIZE)]
    sums = exchanged(sums, along_z)
    after = passed_along(conv, "ctx", -1)
    sums = call(fold_kernel, [((planes, SUM_ROWS, LANES), F32)], (sums,), 1 << 20)[0]
    sums = exchanged(sums, across_z)
    key_grad, value_grad = call(
        functools.partial(backward_kernel, group_size),
        [(wide, BF16)] * 2,
        (conv, after, key_act, value_act, skip_row, bwd),
        4 * rows * rows * width * 8,
    )
    filter_grad, skip_grad = call(
        finish_kernel, [((groups, LANES), F32), ((1, width), F32)], (sums,), 1 << 20
    )
    return gated, query_grad, key_grad, value_grad, filter_grad, skip_grad.reshape(width)


def solution(mesh):
    wide, narrow = P("ctx", "ch"), P("ch", None)

    return jax.shard_map(
        per_device,
        mesh=mesh,
        in_specs=(wide, wide, wide, narrow, P("ch"), narrow, wide),
        out_specs=(wide, wide, wide, wide, narrow, P("ch")),
        check_vma=False,
    )
```

time: 102 us -> 102 us (level)
  the two profiles are of different devices: /device:TPU:2 before, /device:TPU:1 now
where the time goes in v1:
time: 102 us; the launch traced here: 101 us
  starting transfers between devices  45.2 us (44%)
  blocking collectives  21.8 us (21%)
  waiting for transfers between devices  16.3 us (16%)
  Pallas kernels  15.7 us (15%)
    ppermute x3, starting transfers between devices, swap(): return lax.ppermute(block, 'ch', [(c, c ^ 1) for c in range(ch_size)])  24 us
    all_to_all x1, blocking collectives, exchanged(): lax.all_to_all(blocks, 'ctx', 0, 0, axis_index_groups=groups, tiled=True)  21.8 us
    pallas_call x9, Pallas kernels, call(): pl.pallas_call(kernel, out_shape=[jax.ShapeDtypeStruct(s, d) for s, d in...  15.7 us
    all_to_all x1, starting transfers between devices, exchanged(): lax.all_to_all(blocks, 'ctx', 0, 0, axis_index_groups=groups, tiled=True)  11.2 us
    ppermute x3, starting transfers between devices, ring(): return lax.ppermute(block, 'ch', [(c, to(c)) for c in range(ch_size)])  7.3 us
    ppermute x3, waiting for transfers between devices, ring(): return lax.ppermute(block, 'ch', [(c, to(c)) for c in range(ch_size)])  6.75 us
    ppermute x2, waiting for transfers between devices, passed_along(): return lax.ppermute(block, axis, route)  4.93 us
    all_to_all x1, waiting for transfers between devices, exchanged(): lax.all_to_all(blocks, 'ctx', 0, 0, axis_index_groups=groups, tiled=True)  4.58 us
  transfers between devices with their start and end apart: 9, of which 4 were waited for; matrix products, arithmetic and copies ran while one was open for 1% of the time, Pallas kernels for 9%

profile of v1, /device:TPU:1, one launch (start us, length us, event | category | flops | bytes accessed | tf_op | source)
XLA Modules:
  0.0 101.5 jit_solution(7562145562201149473)
XLA Ops:
  0.6 16.0 %collective-permute-start.2 = (bf16[128,1024]{1,0:T(8,128)(2,1)}, bf16[128,1024]{1,0:T(8,128)(2,1)S(1)}, u32[]{:S(2)}, u32[]{:S(2)}) collective-permute-start(bf16[128,1024]{1,0:T(8,128)(2,1)} %own_ref.1), channel_id=1, source_target_pairs={{0,1},{1,0},{2,3},{3,2},{4,5},{5,4},{6,7},{7,6},{8,9},{9,8},{10,11... | collective-permute-start | bytes 786440 | tf_op jit(solution)/shard_map/ppermute | solution.py:248
  16.7 1.9 %collective-permute-start.1 = (bf16[128,1024]{1,0:T(8,128)(2,1)}, bf16[128,1024]{1,0:T(8,128)(2,1)S(1)}, u32[]{:S(2)}, u32[]{:S(2)}) collective-permute-start(bf16[128,1024]{1,0:T(8,128)(2,1)} %own_ref.1), channel_id=1, source_target_pairs={{0,2},{1,7},{2,4},{3,1},{4,6},{5,3},{6,0},{7,5},{8,10},{9,15},{10,... | collective-permute-start | bytes 786440 | tf_op jit(solution)/shard_map/ppermute | solution.py:245
  18.6 1.9 %collective-permute-start.3 = (bf16[128,1024]{1,0:T(8,128)(2,1)S(1)}, bf16[128,1024]{1,0:T(8,128)(2,1)S(1)}, u32[]{:S(2)}, u32[]{:S(2)}) collective-permute-start(bf16[128,1024]{1,0:T(8,128)(2,1)S(1)} %collective-permute-done.2.swap_ref), channel_id=1, source_target_pairs={{0,2},{1,7},{2,4},{3,1},{4,6},{5,3},{6,0},{7,5},{8,10},{9,15},{10,... | collective-permute-start | bytes 786440 | tf_op jit(solution)/shard_map/ppermute | solution.py:245
  20.5 1.0 multiply_convert_fusion.inner_ref
  21.5 0.0 copy-start
  21.6 1.4 %collective-permute-start = (bf16[128,512]{1,0:T(8,128)(2,1)S(1)}, bf16[128,512]{1,0:T(8,128)(2,1)S(1)}, u32[]{:S(2)}, u32[]{:S(2)}) collective-permute-start(bf16[128,512]{1,0:T(8,128)(2,1)S(1)} %multiply_convert_fusion.inner_ref), channel_id=1, source_target_pairs={{0,8},{8,16},{16,24},{24,32},{32,40},{40,48},{48,56},{56,64},{64,7... | collective-permute-start | bytes 393224 | tf_op jit(solution)/shard_map/ppermute | solution.py:227
  23.0 0.0 copy-start.4
  23.0 0.7 copy-done.4
  23.7 2.4 %shard_map.118 = (bf16[32,128,256]{2,1,0:T(8,128)(2,1)S(1)}, bf16[32,128,256]{2,1,0:T(8,128)(2,1)S(1)}, bf16[2,512,1024]{2,1,0:T(8,128)(2,1)S(1)}) custom-call(bf16[32,128]{1,0:T(8,128)(2,1)S(1)} %copy-done.4, bf16[512,8192]{1,0:T(8,128)(2,1)} %weight_hbm.7), custom_call_target="tpu_custom_call" | custom-call | flops 4194304 | bytes 4194304 | tf_op jit(solution)/shard_map/pallas_call | solution.py:213
  26.1 0.0 collective-permute-done.before_ref
  26.1 0.0 collective-permute-done.1.ring1_ref
  26.1 1.9 %collective-permute-done.3.ring2_ref = bf16[128,1024]{1,0:T(8,128)(2,1)S(1)} collective-permute-done((bf16[128,1024]{1,0:T(8,128)(2,1)S(1)}, bf16[128,1024]{1,0:T(8,128)(2,1)S(1)}, u32[]{:S(2)}, u32[]{:S(2)}) %collective-permute-start.3) | collective-permute-done | bytes 262176 | tf_op jit(solution)/shard_map/ppermute | solution.py:245
  28.0 3.0 %shard_map.119 = (f32[128,512]{1,0:T(8,128)S(1)}, bf16[128,512]{1,0:T(8,128)(2,1)}, bf16[368,512]{1,0:T(8,128)(2,1)S(1)}, bf16[2,128,1024]{2,1,0:T(8,128)(2,1)S(1)}, bf16[2,512,1024]{2,1,0:T(8,128)(2,1)S(1)}) custom-call(bf16[128,512]{1,0:T(8,128)(2,1)S(1)} %collective-permute-done.before_ref, bf16[128,512]{1,0:T(8,128)(2,1)S(1)} %multiply_convert_fusion.inner_ref, ...), custom_call_target="tpu_custom_call" | custom-call | flops 268435456 | bytes 4194304 | tf_op jit(solution)/shard_map/pallas_call | solution.py:213
  31.0 4.0 %collective-permute-start.6 = (bf16[2,128,1024]{2,1,0:T(8,128)(2,1)S(1)}, bf16[2,128,1024]{2,1,0:T(8,128)(2,1)S(1)}, u32[]{:S(2)}, u32[]{:S(2)}) collective-permute-start(bf16[2,128,1024]{2,1,0:T(8,128)(2,1)S(1)} %get-tuple-element.31), channel_id=1, source_target_pairs={{0,1},{1,0},{2,3},{3,2},{4,5},{5,4},{6,7},{7,6},{8,9},{9,8},{10,11... | collective-permute-start | bytes 1572872 | tf_op jit(solution)/shard_map/ppermute | solution.py:248
  35.0 3.5 %collective-permute-start.4 = (bf16[128,1024]{1,0:T(8,128)(2,1)S(1)}, bf16[128,1024]{1,0:T(8,128)(2,1)S(1)}, u32[]{:S(2)}, u32[]{:S(2)}) collective-permute-start(bf16[128,1024]{1,0:T(8,128)(2,1)S(1)} %collective-permute-done.1.ring1_ref), channel_id=1, source_target_pairs={{0,2},{1,7},{2,4},{3,1},{4,6},{5,3},{6,0},{7,5},{8,10},{9,15},{10,... | collective-permute-start | bytes 786440 | tf_op jit(solution)/shard_map/ppermute | solution.py:245
  38.4 4.8 %collective-permute-done.4.first_ref = bf16[128,1024]{1,0:T(8,128)(2,1)S(1)} collective-permute-done((bf16[128,1024]{1,0:T(8,128)(2,1)S(1)}, bf16[128,1024]{1,0:T(8,128)(2,1)S(1)}, u32[]{:S(2)}, u32[]{:S(2)}) %collective-permute-start.4) | collective-permute-done | bytes 262176 | tf_op jit(solution)/shard_map/ppermute | solution.py:245
  43.3 4.0 %collective-permute-start.5 = (bf16[128,1024]{1,0:T(8,128)(2,1)S(1)}, bf16[128,1024]{1,0:T(8,128)(2,1)S(1)}, u32[]{:S(2)}, u32[]{:S(2)}) collective-permute-start(bf16[128,1024]{1,0:T(8,128)(2,1)S(1)} %collective-permute-done.4.first_ref), channel_id=1, source_target_pairs={{0,1},{1,0},{2,3},{3,2},{4,5},{5,4},{6,7},{7,6},{8,9},{9,8},{10,11... | collective-permute-start | bytes 786440 | tf_op jit(solution)/shard_map/ppermute | solution.py:248
  47.3 2.3 %shard_map.120 = (f32[128,512]{1,0:T(8,128)S(1)}, bf16[2,512,1024]{2,1,0:T(8,128)(2,1)S(1)}) custom-call(bf16[128,1024]{1,0:T(8,128)(2,1)S(1)} %copy-done.3, bf16[128,1024]{1,0:T(8,128)(2,1)S(1)} %collective-permute-done.2.swap_ref, bf16[2,512,1024]{2,1,0:T(8,128)(2,1)S(1)} %get-tuple-element.27.pair_ref, bf16[512,8192]{1,0:T(8,128)(2,1)} %weight_hbm.7), custom_call_target="tpu_custom_call" | custom-call | flops 268435456 | bytes 4194304 | tf_op jit(solution)/shard_map/pallas_call | solution.py:213
  49.5 2.3 %shard_map.121 = (f32[128,512]{1,0:T(8,128)S(1)}, bf16[2,512,1024]{2,1,0:T(8,128)(2,1)S(1)}) custom-call(bf16[128,1024]{1,0:T(8,128)(2,1)S(1)} %collective-permute-done.1.ring1_ref, bf16[128,1024]{1,0:T(8,128)(2,1)S(1)} %collective-permute-done.3.ring2_ref, bf16[2,512,1024]{2,1,0:T(8,128)(2,1)S(1)} %get-tuple-element.28.pair_ref, ...), custom_call_target="tpu_custom_call" | custom-call | flops 268435456 | bytes 4194304 | tf_op jit(solution)/shard_map/pallas_call | solution.py:213
  51.8 0.8 shard_map.122.acc_ref
  52.7 0.0 collective-permute-done.5.second_ref
  52.7 0.0 copy-start.1
  52.7 0.0 copy-start.2
  52.7 2.2 %shard_map.123 = (bf16[128,512]{1,0:T(8,128)(2,1)S(1)}, bf16[128,512]{1,0:T(8,128)(2,1)}, f32[8,40,128]{2,1,0:T(8,128)S(1)}) custom-call(bf16[2,512,1024]{2,1,0:T(8,128)(2,1)S(1)} %get-tuple-element.30.pair_ref, bf16[128,1024]{1,0:T(8,128)(2,1)S(1)} %collective-permute-done.4.first_ref, bf16[128,1024]{1,0:T(8,128)(2,1)S(1)} %collective-permute-done.5.second_ref, ...), custom_call_target="tpu_custom_call" | custom-call | flops 536870912 | bytes 4194304 | tf_op jit(solution)/shard_map/pallas_call | solution.py:213
  54.9 21.8 %all_to_all.10.got_ref = f32[8,40,128]{2,1,0:T(8,128)S(1)} all-to-all(f32[8,40,128]{2,1,0:T(8,128)S(1)} %get-tuple-element.41), channel_id=1, replica_groups={{0,8,16,24,32,40,48,56},{64,72,80,88,96,104,112,120},{128,136,144,152,1..., dimensions={0} | all-to-all | bytes 327680 | tf_op jit(solution)/shard_map/all_to_all | solution.py:231
  76.6 0.8 shard_map.125
  77.4 11.2 %all-to-all-start.1 = ((f32[16,40,128]{2,1,0:T(8,128)}), f32[16,40,128]{2,1,0:T(8,128)S(1)}, u32[]{:S(2)}, u32[]{:S(2)}) async-start(f32[16,40,128]{2,1,0:T(8,128)} %shard_map.125), calls=%async_computation.1 | async-start | bytes 655360 | tf_op jit(solution)/shard_map/all_to_all | solution.py:231
  88.6 1.3 %collective-permute-start.7 = (bf16[128,512]{1,0:T(8,128)(2,1)S(1)}, bf16[128,512]{1,0:T(8,128)(2,1)S(1)}, u32[]{:S(2)}, u32[]{:S(2)}) collective-permute-start(bf16[128,512]{1,0:T(8,128)(2,1)S(1)} %get-tuple-element.37.conv_ref), channel_id=1, source_target_pairs={{8,0},{16,8},{24,16},{32,24},{40,32},{48,40},{56,48},{64,56},{72,6... | collective-permute-start | bytes 393224 | tf_op jit(solution)/shard_map/ppermute | solution.py:227
  89.9 4.9 %collective-permute-done.7.after_ref = bf16[128,512]{1,0:T(8,128)(2,1)S(1)} collective-permute-done((bf16[128,512]{1,0:T(8,128)(2,1)S(1)}, bf16[128,512]{1,0:T(8,128)(2,1)S(1)}, u32[]{:S(2)}, u32[]{:S(2)}) %collective-permute-start.7) | collective-permute-done | bytes 131104 | tf_op jit(solution)/shard_map/ppermute | solution.py:227
  94.8 1.4 %shard_map.124 = (bf16[128,512]{1,0:T(8,128)(2,1)}, bf16[128,512]{1,0:T(8,128)(2,1)}) custom-call(bf16[128,512]{1,0:T(8,128)(2,1)S(1)} %get-tuple-element.37.conv_ref, bf16[128,512]{1,0:T(8,128)(2,1)S(1)} %collective-permute-done.7.after_ref, bf16[128,512]{1,0:T(8,128)(2,1)S(1)} %copy-done.2, bf16[128,512]{1,0:T(8,128)(2,1)S(1)} %copy-done.1, ...), custom_call_target="tpu_custom_call" | custom-call | flops 268435456 | bytes 4194304 | tf_op jit(solution)/shard_map/pallas_call | solution.py:213
  96.3 4.6 %all-to-all-done.1.got_ref = f32[16,40,128]{2,1,0:T(8,128)S(1)} async-done(((f32[16,40,128]{2,1,0:T(8,128)}), f32[16,40,128]{2,1,0:T(8,128)S(1)}, u32[]{:S(2)}, u32[]{:S(2)}) %all-to-all-start.1) | async-done | bytes 327712 | tf_op jit(solution)/shard_map/all_to_all | solution.py:231
  100.8 0.6 shard_map.126
  (9 shorter events, 0.0 us)
Async XLA Ops:
  0.6 18.0 %collective-permute-start.2 = (bf16[128,1024]{1,0:T(8,128)(2,1)}, bf16[128,1024]{1,0:T(8,128)(2,1)S(1)}, u32[]{:S(2)}, u32[]{:S(2)}) collective-permute-start(bf16[128,1024]{1,0:T(8,128)(2,1)} %own_ref.1), channel_id=1, source_target_pairs={{0,1},{1,0},{2,3},{3,2},{4,5},{5,4},{6,7},{7,6},{8,9},{9,8},{10,11... | collective-permute-start | bytes 786440 | tf_op jit(solution)/shard_map/ppermute | solution.py:248
  16.7 9.4 %collective-permute-start.1 = (bf16[128,1024]{1,0:T(8,128)(2,1)}, bf16[128,1024]{1,0:T(8,128)(2,1)S(1)}, u32[]{:S(2)}, u32[]{:S(2)}) collective-permute-start(bf16[128,1024]{1,0:T(8,128)(2,1)} %own_ref.1), channel_id=1, source_target_pairs={{0,2},{1,7},{2,4},{3,1},{4,6},{5,3},{6,0},{7,5},{8,10},{9,15},{10,... | collective-permute-start | bytes 786440 | tf_op jit(solution)/shard_map/ppermute | solution.py:245
  18.6 9.4 %collective-permute-start.3 = (bf16[128,1024]{1,0:T(8,128)(2,1)S(1)}, bf16[128,1024]{1,0:T(8,128)(2,1)S(1)}, u32[]{:S(2)}, u32[]{:S(2)}) collective-permute-start(bf16[128,1024]{1,0:T(8,128)(2,1)S(1)} %collective-permute-done.2.swap_ref), channel_id=1, source_target_pairs={{0,2},{1,7},{2,4},{3,1},{4,6},{5,3},{6,0},{7,5},{8,10},{9,15},{10,... | collective-permute-start | bytes 786440 | tf_op jit(solution)/shard_map/ppermute | solution.py:245
  21.5 6.5 %copy-start = (bf16[128,512]{1,0:T(8,128)(2,1)S(1)}, bf16[128,512]{1,0:T(8,128)(2,1)}, u32[]{:S(2)}) copy-start(bf16[128,512]{1,0:T(8,128)(2,1)} %query_ref.3) | copy-start | bytes 393220
  21.6 4.5 %collective-permute-start = (bf16[128,512]{1,0:T(8,128)(2,1)S(1)}, bf16[128,512]{1,0:T(8,128)(2,1)S(1)}, u32[]{:S(2)}, u32[]{:S(2)}) collective-permute-start(bf16[128,512]{1,0:T(8,128)(2,1)S(1)} %multiply_convert_fusion.inner_ref), channel_id=1, source_target_pairs={{0,8},{8,16},{16,24},{24,32},{32,40},{40,48},{48,56},{56,64},{64,7... | collective-permute-start | bytes 393224 | tf_op jit(solution)/shard_map/ppermute | solution.py:227
  23.0 0.7 copy-start.4
  23.7 4.3 %copy-start.5 = (f32[512]{0:T(512)S(1)}, f32[512]{0:T(512)}, u32[]{:S(2)}) copy-start(f32[512]{0:T(512)} %param.11) | copy-start | bytes 6148
  28.0 19.3 %copy-start.3 = (bf16[128,1024]{1,0:T(8,128)(2,1)S(1)}, bf16[128,1024]{1,0:T(8,128)(2,1)}, u32[]{:S(2)}) copy-start(bf16[128,1024]{1,0:T(8,128)(2,1)} %own_ref.1) | copy-start | bytes 786436
  31.0 20.8 %collective-permute-start.6 = (bf16[2,128,1024]{2,1,0:T(8,128)(2,1)S(1)}, bf16[2,128,1024]{2,1,0:T(8,128)(2,1)S(1)}, u32[]{:S(2)}, u32[]{:S(2)}) collective-permute-start(bf16[2,128,1024]{2,1,0:T(8,128)(2,1)S(1)} %get-tuple-element.31), channel_id=1, source_target_pairs={{0,1},{1,0},{2,3},{3,2},{4,5},{5,4},{6,7},{7,6},{8,9},{9,8},{10,11... | collective-permute-start | bytes 1572872 | tf_op jit(solution)/shard_map/ppermute | solution.py:248
  35.0 8.3 %collective-permute-start.4 = (bf16[128,1024]{1,0:T(8,128)(2,1)S(1)}, bf16[128,1024]{1,0:T(8,128)(2,1)S(1)}, u32[]{:S(2)}, u32[]{:S(2)}) collective-permute-start(bf16[128,1024]{1,0:T(8,128)(2,1)S(1)} %collective-permute-done.1.ring1_ref), channel_id=1, source_target_pairs={{0,2},{1,7},{2,4},{3,1},{4,6},{5,3},{6,0},{7,5},{8,10},{9,15},{10,... | collective-permute-start | bytes 786440 | tf_op jit(solution)/shard_map/ppermute | solution.py:245
  43.3 9.4 %collective-permute-start.5 = (bf16[128,1024]{1,0:T(8,128)(2,1)S(1)}, bf16[128,1024]{1,0:T(8,128)(2,1)S(1)}, u32[]{:S(2)}, u32[]{:S(2)}) collective-permute-start(bf16[128,1024]{1,0:T(8,128)(2,1)S(1)} %collective-permute-done.4.first_ref), channel_id=1, source_target_pairs={{0,1},{1,0},{2,3},{3,2},{4,5},{5,4},{6,7},{7,6},{8,9},{9,8},{10,11... | collective-permute-start | bytes 786440 | tf_op jit(solution)/shard_map/ppermute | solution.py:248
  52.7 42.2 %copy-start.1 = (bf16[128,512]{1,0:T(8,128)(2,1)S(1)}, bf16[128,512]{1,0:T(8,128)(2,1)}, u32[]{:S(2)}) copy-start(bf16[128,512]{1,0:T(8,128)(2,1)} %value_ref.1) | copy-start | bytes 393220
  52.7 42.2 %copy-start.2 = (bf16[128,512]{1,0:T(8,128)(2,1)S(1)}, bf16[128,512]{1,0:T(8,128)(2,1)}, u32[]{:S(2)}) copy-start(bf16[128,512]{1,0:T(8,128)(2,1)} %key_ref.1) | copy-start | bytes 393220
  77.4 23.4 %all-to-all-start.1 = ((f32[16,40,128]{2,1,0:T(8,128)}), f32[16,40,128]{2,1,0:T(8,128)S(1)}, u32[]{:S(2)}, u32[]{:S(2)}) async-start(f32[16,40,128]{2,1,0:T(8,128)} %shard_map.125), calls=%async_computation.1 | async-start | bytes 655360 | tf_op jit(solution)/shard_map/all_to_all | solution.py:231
  88.6 6.2 %collective-permute-start.7 = (bf16[128,512]{1,0:T(8,128)(2,1)S(1)}, bf16[128,512]{1,0:T(8,128)(2,1)S(1)}, u32[]{:S(2)}, u32[]{:S(2)}) collective-permute-start(bf16[128,512]{1,0:T(8,128)(2,1)S(1)} %get-tuple-element.37.conv_ref), channel_id=1, source_target_pairs={{8,0},{16,8},{24,16},{32,24},{40,32},{48,40},{56,48},{64,56},{72,6... | collective-permute-start | bytes 393224 | tf_op jit(solution)/shard_map/ppermute | solution.py:227

commit v2 on v1

--- a/solution.py
+++ b/solution.py
@@ -14,7 +14,8 @@
 Z_SIZE = 8
 CORES = 2
 SUM_ROWS = 40
-VMEM_MIB = 44
+PIECES = 4
+VMEM_MIB = 42
 PAIR_DISTANCE = (0, -1, 1, 2)
 SWAPPED_PAIR = 2
 
@@ -69,13 +70,15 @@
 
 def fetched(weight_hbm, pair_ref, sem, pair):
     depth = pair_ref.shape[2]
+    height = pair_ref.shape[1] // PIECES
     copies = []
     for i, position in enumerate(positions(pair)):
         columns = pl.ds(pl.multiple_of(position * depth, depth), depth)
-        copies.append(
-            pltpu.make_async_copy(weight_hbm.at[:, columns], pair_ref.at[i], sem.at[i])
-        )
-        copies[-1].start()
+        for j in range(PIECES):
+            rows = pl.ds(j * height, height)
+            source, target = weight_hbm.at[rows, columns], pair_ref.at[i, rows]
+            copies.append(pltpu.make_async_copy(source, target, sem.at[i * PIECES + j]))
+            copies[-1].start()
     return copies
 
 
@@ -84,8 +87,13 @@
         copy.wait()
 
 
-def stage_kernel(filt_ref, weight_hbm, fwd_ref, bwd_ref, pair_ref, sem):
-    copies = fetched(weight_hbm, pair_ref, sem, 0)
+def stage_kernel(filt_hbm, weight_hbm, fwd_ref, bwd_ref, pair0_ref, pair1_ref,
+                 filt_ref, filt_sem, sem0, sem1):
+    load = pltpu.make_async_copy(filt_hbm, filt_ref, filt_sem)
+    load.start()
+    copies = fetched(weight_hbm, pair0_ref, sem0, 0)
+    copies += fetched(weight_hbm, pair1_ref, sem1, 1)
+    load.wait()
     groups, taps = filt_ref.shape
     filt = filt_ref[...]
     flipped = dot(filt, reversal(taps))
@@ -127,10 +135,8 @@
     return total
 
 
-def first_product_kernel(own_ref, swap_ref, pair_ref, weight_hbm, out_ref, next_ref, sem):
-    copies = fetched(weight_hbm, next_ref, sem, 1)
+def first_product_kernel(own_ref, swap_ref, pair_ref, out_ref):
     out_ref[...] = products((own_ref[...], swap_ref[...]), pair_ref)
-    finished(copies)
 
 
 def second_product_kernel(ring1_ref, ring2_ref, pair_ref, acc_ref, weight_hbm,
@@ -253,30 +259,27 @@
     hbm = pl.BlockSpec(memory_space=pltpu.HBM)
     pair = ((2, width, depth), BF16)
     wide = (rows, width)
-    sem = [pltpu.SemaphoreType.DMA((2,))]
+    sem = [pltpu.SemaphoreType.DMA((2 * PIECES,))]
 
     ring1 = ring(out_grad)
     swap0 = swap(out_grad)
     before = passed_along(inner, "ctx", 1)
     ring2 = ring(swap0)
-    fwd, bwd, pair0 = call(
+    fwd, bwd, pair0, pair1 = call(
         stage_kernel,
-        [((groups, taps, 2 * taps), BF16)] * 2 + [pair],
+        [((groups, taps, 2 * taps), BF16)] * 2 + [pair] * 2,
         (filters, out_weight),
         8 * groups * taps * taps,
-        [VMEM_SPEC, hbm],
-        sem,
+        [hbm, hbm],
+        [pltpu.VMEM(filters.shape, BF16), pltpu.SemaphoreType.DMA] + sem * 2,
         VMEM_MIB,
     )
-    acc, pair1 = call(
+    acc = call(
         first_product_kernel,
-        [(wide, F32), pair],
-        (out_grad, swap0, pair0, out_weight),
+        [(wide, F32)],
+        (out_grad, swap0, pair0),
         4 * rows * depth * width,
-        [VMEM_SPEC] * 3 + [hbm],
-        sem,
-        VMEM_MIB,
-    )
+    )[0]
     ring3 = ring(ring1)
     mixed, gated, flipped, packed, pair2 = call(
         functools.partial(forward_kernel, group_size),
@@ -299,7 +302,10 @@
     )
     swap3 = swap(ring3)
     acc = call(
-        third_product_kernel, [(wide, F32)], (swap12, pair2, acc), 4 * rows * depth * width
+        third_product_kernel,
+        [(wide, F32)],
+        (swap12, pair2, acc),
+        4 * rows * depth * width,
     )[0]
     planes = ctx_size // Z_SIZE
     conv, query_grad, sums = call(

time: 102 us -> 101 us (level)
  Pallas kernels: 15.7 us -> 14.2 us
    pallas_call x9, Pallas kernels: 15.7 us -> 14.2 us  [call(): pl.pallas_call(kernel, out_shape=[jax.ShapeDtypeStruct(s, d) for s, d in...]
  transfers between devices with their start and end apart: 9 -> 9, of which waited for: 4 -> 5; matrix products, arithmetic and copies ran while one was open for 1% -> 1% of each run, Pallas kernels for 9% -> 8%
where the time goes in v2:
time: 101 us; the launch traced here: 100 us
  starting transfers between devices  45.2 us (45%)
  blocking collectives  21.8 us (22%)
  waiting for transfers between devices  16.3 us (16%)
  Pallas kernels  14.2 us (14%)
    ppermute x3, starting transfers between devices, swap(): return lax.ppermute(block, 'ch', [(c, c ^ 1) for c in range(ch_size)])  24 us
    all_to_all x1, blocking collectives, exchanged(): lax.all_to_all(blocks, 'ctx', 0, 0, axis_index_groups=groups, tiled=True)  21.8 us
    pallas_call x9, Pallas kernels, call(): pl.pallas_call(kernel, out_shape=[jax.ShapeDtypeStruct(s, d) for s, d in...  14.2 us
    all_to_all x1, starting transfers between devices, exchanged(): lax.all_to_all(blocks, 'ctx', 0, 0, axis_index_groups=groups, tiled=True)  11.2 us
    ppermute x3, starting transfers between devices, ring(): return lax.ppermute(block, 'ch', [(c, to(c)) for c in range(ch_size)])  7.3 us
    ppermute x3, waiting for transfers between devices, ring(): return lax.ppermute(block, 'ch', [(c, to(c)) for c in range(ch_size)])  6.75 us
    ppermute x2, waiting for transfers between devices, passed_along(): return lax.ppermute(block, axis, route)  5 us
    all_to_all x1, waiting for transfers between devices, exchanged(): lax.all_to_all(blocks, 'ctx', 0, 0, axis_index_groups=groups, tiled=True)  4.58 us
  transfers between devices with their start and end apart: 9, of which 5 were waited for; matrix products, arithmetic and copies ran while one was open for 1% of the time, Pallas kernels for 8%

profile of v2, /device:TPU:1, one launch (start us, length us, event | category | flops | bytes accessed | tf_op | source)
XLA Modules:
  0.0 100.1 jit_solution(15806069561713318389)
XLA Ops:
  0.6 16.0 %collective-permute-start.2 = (bf16[128,1024]{1,0:T(8,128)(2,1)}, bf16[128,1024]{1,0:T(8,128)(2,1)S(1)}, u32[]{:S(2)}, u32[]{:S(2)}) collective-permute-start(bf16[128,1024]{1,0:T(8,128)(2,1)} %own_ref.1), channel_id=1, source_target_pairs={{0,1},{1,0},{2,3},{3,2},{4,5},{5,4},{6,7},{7,6},{8,9},{9,8},{10,11... | collective-permute-start | bytes 786440 | tf_op jit(solution)/shard_map/ppermute | solution.py:254
  16.7 1.9 %collective-permute-start.1 = (bf16[128,1024]{1,0:T(8,128)(2,1)}, bf16[128,1024]{1,0:T(8,128)(2,1)S(1)}, u32[]{:S(2)}, u32[]{:S(2)}) collective-permute-start(bf16[128,1024]{1,0:T(8,128)(2,1)} %own_ref.1), channel_id=1, source_target_pairs={{0,2},{1,7},{2,4},{3,1},{4,6},{5,3},{6,0},{7,5},{8,10},{9,15},{10,... | collective-permute-start | bytes 786440 | tf_op jit(solution)/shard_map/ppermute | solution.py:251
  18.6 1.9 %collective-permute-start.3 = (bf16[128,1024]{1,0:T(8,128)(2,1)S(1)}, bf16[128,1024]{1,0:T(8,128)(2,1)S(1)}, u32[]{:S(2)}, u32[]{:S(2)}) collective-permute-start(bf16[128,1024]{1,0:T(8,128)(2,1)S(1)} %collective-permute-done.2.swap_ref), channel_id=1, source_target_pairs={{0,2},{1,7},{2,4},{3,1},{4,6},{5,3},{6,0},{7,5},{8,10},{9,15},{10,... | collective-permute-start | bytes 786440 | tf_op jit(solution)/shard_map/ppermute | solution.py:251
  20.5 1.0 %multiply_convert_fusion.inner_ref = bf16[128,512]{1,0:T(8,128)(2,1)S(1)} fusion(bf16[128,512]{1,0:T(8,128)(2,1)} %value_ref.1, bf16[128,512]{1,0:T(8,128)(2,1)} %key_ref.1), kind=kLoop, calls=%fused_computation | loop fusion | flops 262144 | bytes 393216 | tf_op jit(solution)/shard_map/convert_element_type | solution.py:257
  21.5 0.0 copy-start
  21.6 1.4 %collective-permute-start = (bf16[128,512]{1,0:T(8,128)(2,1)S(1)}, bf16[128,512]{1,0:T(8,128)(2,1)S(1)}, u32[]{:S(2)}, u32[]{:S(2)}) collective-permute-start(bf16[128,512]{1,0:T(8,128)(2,1)S(1)} %multiply_convert_fusion.inner_ref), channel_id=1, source_target_pairs={{0,8},{8,16},{16,24},{24,32},{32,40},{40,48},{48,56},{56,64},{64,7... | collective-permute-start | bytes 393224 | tf_op jit(solution)/shard_map/ppermute | solution.py:233
  23.0 0.0 copy-start.4
  23.0 0.7 copy-done.4
  23.7 2.3 %shard_map.118 = (bf16[32,128,256]{2,1,0:T(8,128)(2,1)S(1)}, bf16[32,128,256]{2,1,0:T(8,128)(2,1)S(1)}, bf16[2,512,1024]{2,1,0:T(8,128)(2,1)S(1)}, bf16[2,512,1024]{2,1,0:T(8,128)(2,1)S(1)}) custom-call(bf16[32,128]{1,0:T(8,128)(2,1)S(1)} %copy-done.4, bf16[512,8192]{1,0:T(8,128)(2,1)} %weight_hbm.5), custom_call_target="tpu_custom_call" | custom-call | flops 4194304 | bytes 4194304 | tf_op jit(solution)/shard_map/pallas_call | solution.py:219
  26.0 0.1 collective-permute-done.before_ref
  26.1 0.0 collective-permute-done.1.ring1_ref
  26.1 1.9 %collective-permute-done.3.ring2_ref = bf16[128,1024]{1,0:T(8,128)(2,1)S(1)} collective-permute-done((bf16[128,1024]{1,0:T(8,128)(2,1)S(1)}, bf16[128,1024]{1,0:T(8,128)(2,1)S(1)}, u32[]{:S(2)}, u32[]{:S(2)}) %collective-permute-start.3) | collective-permute-done | bytes 262176 | tf_op jit(solution)/shard_map/ppermute | solution.py:251
  28.0 3.0 %shard_map.119 = (f32[128,512]{1,0:T(8,128)S(1)}, bf16[128,512]{1,0:T(8,128)(2,1)}, bf16[368,512]{1,0:T(8,128)(2,1)S(1)}, bf16[2,128,1024]{2,1,0:T(8,128)(2,1)S(1)}, bf16[2,512,1024]{2,1,0:T(8,128)(2,1)S(1)}) custom-call(bf16[128,512]{1,0:T(8,128)(2,1)S(1)} %collective-permute-done.before_ref, bf16[128,512]{1,0:T(8,128)(2,1)S(1)} %multiply_convert_fusion.inner_ref, ...), custom_call_target="tpu_custom_call" | custom-call | flops 268435456 | bytes 4194304 | tf_op jit(solution)/shard_map/pallas_call | solution.py:219
  31.0 4.0 %collective-permute-start.6 = (bf16[2,128,1024]{2,1,0:T(8,128)(2,1)S(1)}, bf16[2,128,1024]{2,1,0:T(8,128)(2,1)S(1)}, u32[]{:S(2)}, u32[]{:S(2)}) collective-permute-start(bf16[2,128,1024]{2,1,0:T(8,128)(2,1)S(1)} %get-tuple-element.29), channel_id=1, source_target_pairs={{0,1},{1,0},{2,3},{3,2},{4,5},{5,4},{6,7},{7,6},{8,9},{9,8},{10,11... | collective-permute-start | bytes 1572872 | tf_op jit(solution)/shard_map/ppermute | solution.py:254
  35.0 3.5 %collective-permute-start.4 = (bf16[128,1024]{1,0:T(8,128)(2,1)S(1)}, bf16[128,1024]{1,0:T(8,128)(2,1)S(1)}, u32[]{:S(2)}, u32[]{:S(2)}) collective-permute-start(bf16[128,1024]{1,0:T(8,128)(2,1)S(1)} %collective-permute-done.1.ring1_ref), channel_id=1, source_target_pairs={{0,2},{1,7},{2,4},{3,1},{4,6},{5,3},{6,0},{7,5},{8,10},{9,15},{10,... | collective-permute-start | bytes 786440 | tf_op jit(solution)/shard_map/ppermute | solution.py:251
  38.4 4.8 %collective-permute-done.4.first_ref = bf16[128,1024]{1,0:T(8,128)(2,1)S(1)} collective-permute-done((bf16[128,1024]{1,0:T(8,128)(2,1)S(1)}, bf16[128,1024]{1,0:T(8,128)(2,1)S(1)}, u32[]{:S(2)}, u32[]{:S(2)}) %collective-permute-start.4) | collective-permute-done | bytes 262176 | tf_op jit(solution)/shard_map/ppermute | solution.py:251
  43.3 4.0 %collective-permute-start.5 = (bf16[128,1024]{1,0:T(8,128)(2,1)S(1)}, bf16[128,1024]{1,0:T(8,128)(2,1)S(1)}, u32[]{:S(2)}, u32[]{:S(2)}) collective-permute-start(bf16[128,1024]{1,0:T(8,128)(2,1)S(1)} %collective-permute-done.4.first_ref), channel_id=1, source_target_pairs={{0,1},{1,0},{2,3},{3,2},{4,5},{5,4},{6,7},{7,6},{8,9},{9,8},{10,11... | collective-permute-start | bytes 786440 | tf_op jit(solution)/shard_map/ppermute | solution.py:254
  47.3 0.8 shard_map.120.acc_ref
  48.1 2.3 %shard_map.121 = (f32[128,512]{1,0:T(8,128)S(1)}, bf16[2,512,1024]{2,1,0:T(8,128)(2,1)S(1)}) custom-call(bf16[128,1024]{1,0:T(8,128)(2,1)S(1)} %collective-permute-done.1.ring1_ref, bf16[128,1024]{1,0:T(8,128)(2,1)S(1)} %collective-permute-done.3.ring2_ref, bf16[2,512,1024]{2,1,0:T(8,128)(2,1)S(1)} %get-tuple-element.26.pair_ref, ...), custom_call_target="tpu_custom_call" | custom-call | flops 268435456 | bytes 4194304 | tf_op jit(solution)/shard_map/pallas_call | solution.py:219
  50.4 0.8 shard_map.122.acc_ref
  51.2 0.0 collective-permute-done.5.second_ref
  51.3 0.0 copy-start.1
  51.3 0.0 copy-start.2
  51.3 2.2 %shard_map.123 = (bf16[128,512]{1,0:T(8,128)(2,1)S(1)}, bf16[128,512]{1,0:T(8,128)(2,1)}, f32[8,40,128]{2,1,0:T(8,128)S(1)}) custom-call(bf16[2,512,1024]{2,1,0:T(8,128)(2,1)S(1)} %get-tuple-element.28.pair_ref, bf16[128,1024]{1,0:T(8,128)(2,1)S(1)} %collective-permute-done.4.first_ref, bf16[128,1024]{1,0:T(8,128)(2,1)S(1)} %collective-permute-done.5.second_ref, ...), custom_call_target="tpu_custom_call" | custom-call | flops 536870912 | bytes 4194304 | tf_op jit(solution)/shard_map/pallas_call | solution.py:219
  53.5 21.8 %all_to_all.10.got_ref = f32[8,40,128]{2,1,0:T(8,128)S(1)} all-to-all(f32[8,40,128]{2,1,0:T(8,128)S(1)} %get-tuple-element.39), channel_id=1, replica_groups={{0,8,16,24,32,40,48,56},{64,72,80,88,96,104,112,120},{128,136,144,152,1..., dimensions={0} | all-to-all | bytes 327680 | tf_op jit(solution)/shard_map/all_to_all | solution.py:237
  75.3 0.8 shard_map.125
  76.0 11.2 %all-to-all-start.1 = ((f32[16,40,128]{2,1,0:T(8,128)}), f32[16,40,128]{2,1,0:T(8,128)S(1)}, u32[]{:S(2)}, u32[]{:S(2)}) async-start(f32[16,40,128]{2,1,0:T(8,128)} %shard_map.125), calls=%async_computation.1 | async-start | bytes 655360 | tf_op jit(solution)/shard_map/all_to_all | solution.py:237
  87.2 1.3 %collective-permute-start.7 = (bf16[128,512]{1,0:T(8,128)(2,1)S(1)}, bf16[128,512]{1,0:T(8,128)(2,1)S(1)}, u32[]{:S(2)}, u32[]{:S(2)}) collective-permute-start(bf16[128,512]{1,0:T(8,128)(2,1)S(1)} %get-tuple-element.35.conv_ref), channel_id=1, source_target_pairs={{8,0},{16,8},{24,16},{32,24},{40,32},{48,40},{56,48},{64,56},{72,6... | collective-permute-start | bytes 393224 | tf_op jit(solution)/shard_map/ppermute | solution.py:233
  88.5 4.9 %collective-permute-done.7.after_ref = bf16[128,512]{1,0:T(8,128)(2,1)S(1)} collective-permute-done((bf16[128,512]{1,0:T(8,128)(2,1)S(1)}, bf16[128,512]{1,0:T(8,128)(2,1)S(1)}, u32[]{:S(2)}, u32[]{:S(2)}) %collective-permute-start.7) | collective-permute-done | bytes 131104 | tf_op jit(solution)/shard_map/ppermute | solution.py:233
  93.5 1.4 %shard_map.124 = (bf16[128,512]{1,0:T(8,128)(2,1)}, bf16[128,512]{1,0:T(8,128)(2,1)}) custom-call(bf16[128,512]{1,0:T(8,128)(2,1)S(1)} %get-tuple-element.35.conv_ref, bf16[128,512]{1,0:T(8,128)(2,1)S(1)} %collective-permute-done.7.after_ref, bf16[128,512]{1,0:T(8,128)(2,1)S(1)} %copy-done.2, bf16[128,512]{1,0:T(8,128)(2,1)S(1)} %copy-done.1, ...), custom_call_target="tpu_custom_call" | custom-call | flops 268435456 | bytes 4194304 | tf_op jit(solution)/shard_map/pallas_call | solution.py:219
  94.9 4.6 %all-to-all-done.1.got_ref = f32[16,40,128]{2,1,0:T(8,128)S(1)} async-done(((f32[16,40,128]{2,1,0:T(8,128)}), f32[16,40,128]{2,1,0:T(8,128)S(1)}, u32[]{:S(2)}, u32[]{:S(2)}) %all-to-all-start.1) | async-done | bytes 327712 | tf_op jit(solution)/shard_map/all_to_all | solution.py:237
  99.5 0.6 shard_map.126
  (9 shorter events, 0.0 us)
Async XLA Ops:
  0.6 18.0 %collective-permute-start.2 = (bf16[128,1024]{1,0:T(8,128)(2,1)}, bf16[128,1024]{1,0:T(8,128)(2,1)S(1)}, u32[]{:S(2)}, u32[]{:S(2)}) collective-permute-start(bf16[128,1024]{1,0:T(8,128)(2,1)} %own_ref.1), channel_id=1, source_target_pairs={{0,1},{1,0},{2,3},{3,2},{4,5},{5,4},{6,7},{7,6},{8,9},{9,8},{10,11... | collective-permute-start | bytes 786440 | tf_op jit(solution)/shard_map/ppermute | solution.py:254
  16.7 9.4 %collective-permute-start.1 = (bf16[128,1024]{1,0:T(8,128)(2,1)}, bf16[128,1024]{1,0:T(8,128)(2,1)S(1)}, u32[]{:S(2)}, u32[]{:S(2)}) collective-permute-start(bf16[128,1024]{1,0:T(8,128)(2,1)} %own_ref.1), channel_id=1, source_target_pairs={{0,2},{1,7},{2,4},{3,1},{4,6},{5,3},{6,0},{7,5},{8,10},{9,15},{10,... | collective-permute-start | bytes 786440 | tf_op jit(solution)/shard_map/ppermute | solution.py:251
  18.6 9.4 %collective-permute-start.3 = (bf16[128,1024]{1,0:T(8,128)(2,1)S(1)}, bf16[128,1024]{1,0:T(8,128)(2,1)S(1)}, u32[]{:S(2)}, u32[]{:S(2)}) collective-permute-start(bf16[128,1024]{1,0:T(8,128)(2,1)S(1)} %collective-permute-done.2.swap_ref), channel_id=1, source_target_pairs={{0,2},{1,7},{2,4},{3,1},{4,6},{5,3},{6,0},{7,5},{8,10},{9,15},{10,... | collective-permute-start | bytes 786440 | tf_op jit(solution)/shard_map/ppermute | solution.py:251
  21.5 6.5 %copy-start = (bf16[128,512]{1,0:T(8,128)(2,1)S(1)}, bf16[128,512]{1,0:T(8,128)(2,1)}, u32[]{:S(2)}) copy-start(bf16[128,512]{1,0:T(8,128)(2,1)} %query_ref.3) | copy-start | bytes 393220
  21.6 4.5 %collective-permute-start = (bf16[128,512]{1,0:T(8,128)(2,1)S(1)}, bf16[128,512]{1,0:T(8,128)(2,1)S(1)}, u32[]{:S(2)}, u32[]{:S(2)}) collective-permute-start(bf16[128,512]{1,0:T(8,128)(2,1)S(1)} %multiply_convert_fusion.inner_ref), channel_id=1, source_target_pairs={{0,8},{8,16},{16,24},{24,32},{32,40},{40,48},{48,56},{56,64},{64,7... | collective-permute-start | bytes 393224 | tf_op jit(solution)/shard_map/ppermute | solution.py:233
  23.0 0.7 copy-start.4
  23.7 4.3 %copy-start.5 = (f32[512]{0:T(512)S(1)}, f32[512]{0:T(512)}, u32[]{:S(2)}) copy-start(f32[512]{0:T(512)} %param.11) | copy-start | bytes 6148
  28.0 19.3 %copy-start.3 = (bf16[128,1024]{1,0:T(8,128)(2,1)S(1)}, bf16[128,1024]{1,0:T(8,128)(2,1)}, u32[]{:S(2)}) copy-start(bf16[128,1024]{1,0:T(8,128)(2,1)} %own_ref.1) | copy-start | bytes 786436
  31.0 19.4 %collective-permute-start.6 = (bf16[2,128,1024]{2,1,0:T(8,128)(2,1)S(1)}, bf16[2,128,1024]{2,1,0:T(8,128)(2,1)S(1)}, u32[]{:S(2)}, u32[]{:S(2)}) collective-permute-start(bf16[2,128,1024]{2,1,0:T(8,128)(2,1)S(1)} %get-tuple-element.29), channel_id=1, source_target_pairs={{0,1},{1,0},{2,3},{3,2},{4,5},{5,4},{6,7},{7,6},{8,9},{9,8},{10,11... | collective-permute-start | bytes 1572872 | tf_op jit(solution)/shard_map/ppermute | solution.py:254
  35.0 8.3 %collective-permute-start.4 = (bf16[128,1024]{1,0:T(8,128)(2,1)S(1)}, bf16[128,1024]{1,0:T(8,128)(2,1)S(1)}, u32[]{:S(2)}, u32[]{:S(2)}) collective-permute-start(bf16[128,1024]{1,0:T(8,128)(2,1)S(1)} %collective-permute-done.1.ring1_ref), channel_id=1, source_target_pairs={{0,2},{1,7},{2,4},{3,1},{4,6},{5,3},{6,0},{7,5},{8,10},{9,15},{10,... | collective-permute-start | bytes 786440 | tf_op jit(solution)/shard_map/ppermute | solution.py:251
  43.3 8.0 %collective-permute-start.5 = (bf16[128,1024]{1,0:T(8,128)(2,1)S(1)}, bf16[128,1024]{1,0:T(8,128)(2,1)S(1)}, u32[]{:S(2)}, u32[]{:S(2)}) collective-permute-start(bf16[128,1024]{1,0:T(8,128)(2,1)S(1)} %collective-permute-done.4.first_ref), channel_id=1, source_target_pairs={{0,1},{1,0},{2,3},{3,2},{4,5},{5,4},{6,7},{7,6},{8,9},{9,8},{10,11... | collective-permute-start | bytes 786440 | tf_op jit(solution)/shard_map/ppermute | solution.py:254
  51.3 42.2 %copy-start.1 = (bf16[128,512]{1,0:T(8,128)(2,1)S(1)}, bf16[128,512]{1,0:T(8,128)(2,1)}, u32[]{:S(2)}) copy-start(bf16[128,512]{1,0:T(8,128)(2,1)} %value_ref.1) | copy-start | bytes 393220
  51.3 42.2 %copy-start.2 = (bf16[128,512]{1,0:T(8,128)(2,1)S(1)}, bf16[128,512]{1,0:T(8,128)(2,1)}, u32[]{:S(2)}) copy-start(bf16[128,512]{1,0:T(8,128)(2,1)} %key_ref.1) | copy-start | bytes 393220
  76.0 23.5 %all-to-all-start.1 = ((f32[16,40,128]{2,1,0:T(8,128)}), f32[16,40,128]{2,1,0:T(8,128)S(1)}, u32[]{:S(2)}, u32[]{:S(2)}) async-start(f32[16,40,128]{2,1,0:T(8,128)} %shard_map.125), calls=%async_computation.1 | async-start | bytes 655360 | tf_op jit(solution)/shard_map/all_to_all | solution.py:237
  87.2 6.2 %collective-permute-start.7 = (bf16[128,512]{1,0:T(8,128)(2,1)S(1)}, bf16[128,512]{1,0:T(8,128)(2,1)S(1)}, u32[]{:S(2)}, u32[]{:S(2)}) collective-permute-start(bf16[128,512]{1,0:T(8,128)(2,1)S(1)} %get-tuple-element.35.conv_ref), channel_id=1, source_target_pairs={{8,0},{16,8},{24,16},{32,24},{40,32},{48,40},{56,48},{64,56},{72,6... | collective-permute-start | bytes 393224 | tf_op jit(solution)/shard_map/ppermute | solution.py:233

commit v3 on v2

--- a/solution.py
+++ b/solution.py
@@ -14,7 +14,6 @@
 Z_SIZE = 8
 CORES = 2
 SUM_ROWS = 40
-PIECES = 4
 VMEM_MIB = 42
 PAIR_DISTANCE = (0, -1, 1, 2)
 SWAPPED_PAIR = 2
@@ -68,32 +67,24 @@
     return [owner * CORES + first, owner * CORES + 1 - first]
 
 
-def fetched(weight_hbm, pair_ref, sem, pair):
-    depth = pair_ref.shape[2]
-    height = pair_ref.shape[1] // PIECES
+def load_kernel(weight_hbm, blocks_ref, sem):
+    depth = blocks_ref.shape[2]
     copies = []
-    for i, position in enumerate(positions(pair)):
-        columns = pl.ds(pl.multiple_of(position * depth, depth), depth)
-        for j in range(PIECES):
-            rows = pl.ds(j * height, height)
-            source, target = weight_hbm.at[rows, columns], pair_ref.at[i, rows]
-            copies.append(pltpu.make_async_copy(source, target, sem.at[i * PIECES + j]))
+    for pair in range(len(PAIR_DISTANCE)):
+        for i, position in enumerate(positions(pair)):
+            columns = pl.ds(pl.multiple_of(position * depth, depth), depth)
+            slot = 2 * pair + i
+            copies.append(
+                pltpu.make_async_copy(
+                    weight_hbm.at[:, columns], blocks_ref.at[slot], sem.at[slot]
+                )
+            )
             copies[-1].start()
-    return copies
-
-
-def finished(copies):
     for copy in copies:
         copy.wait()
 
 
-def stage_kernel(filt_hbm, weight_hbm, fwd_ref, bwd_ref, pair0_ref, pair1_ref,
-                 filt_ref, filt_sem, sem0, sem1):
-    load = pltpu.make_async_copy(filt_hbm, filt_ref, filt_sem)
-    load.start()
-    copies = fetched(weight_hbm, pair0_ref, sem0, 0)
-    copies += fetched(weight_hbm, pair1_ref, sem1, 1)
-    load.wait()
+def tables_kernel(filt_ref, fwd_ref, bwd_ref):
     groups, taps = filt_ref.shape
     filt = filt_ref[...]
     flipped = dot(filt, reversal(taps))
@@ -106,13 +97,10 @@
             out_ref[g] = pltpu.roll(
                 full, first, axis=1, stride=1, stride_axis=0
             ).astype(BF16)
-    finished(copies)
 
 
 def forward_kernel(group_size, before_ref, inner_ref, query_ref, skip_ref, fwd_ref,
-                   ring1_ref, ring2_ref, weight_hbm,
-                   mixed_ref, gated_ref, flipped_ref, packed_ref, pair_ref, sem):
-    copies = fetched(weight_hbm, pair_ref, sem, 2)
+                   ring1_ref, ring2_ref, mixed_ref, gated_ref, flipped_ref, packed_ref):
     packed_ref[0] = ring1_ref[...]
     packed_ref[1] = ring2_ref[...]
     rows = inner_ref.shape[0]
@@ -124,37 +112,34 @@
     gated_ref[...] = (query_ref[...].astype(F32) * mixed).astype(BF16)
     flipped_ref[:rows - 16] = jnp.zeros((rows - 16, inner.shape[1]), BF16)
     flipped_ref[rows - 16 :] = dot(reversal(2 * rows), series).astype(BF16)
-    finished(copies)
-
-
-def products(blocks, pair_ref):
+
+
+def products(received, blocks_ref, pair):
     total = None
-    for i, block in enumerate(blocks):
-        term = lax.dot_general(block, pair_ref[i], NT, preferred_element_type=F32)
+    for i, block in enumerate(received):
+        weight = blocks_ref[2 * pair + i]
+        term = lax.dot_general(block, weight, NT, preferred_element_type=F32)
         total = term if total is None else total + term
     return total
 
 
-def first_product_kernel(own_ref, swap_ref, pair_ref, out_ref):
-    out_ref[...] = products((own_ref[...], swap_ref[...]), pair_ref)
-
-
-def second_product_kernel(ring1_ref, ring2_ref, pair_ref, acc_ref, weight_hbm,
-                          out_ref, next_ref, sem):
-    copies = fetched(weight_hbm, next_ref, sem, 3)
-    out_ref[...] = acc_ref[...] + products((ring1_ref[...], ring2_ref[...]), pair_ref)
-    finished(copies)
-
-
-def third_product_kernel(swaps_ref, pair_ref, acc_ref, out_ref):
-    out_ref[...] = acc_ref[...] + products((swaps_ref[0], swaps_ref[1]), pair_ref)
-
-
-def gradient_kernel(group_size, pair_ref, first_ref, second_ref, acc_ref,
+def first_product_kernel(own_ref, swap_ref, blocks_ref, out_ref):
+    out_ref[...] = products((own_ref[...], swap_ref[...]), blocks_ref, 0)
+
+
+def second_product_kernel(ring1_ref, ring2_ref, blocks_ref, acc_ref, out_ref):
+    out_ref[...] = acc_ref[...] + products((ring1_ref[...], ring2_ref[...]), blocks_ref, 1)
+
+
+def third_product_kernel(swaps_ref, blocks_ref, acc_ref, out_ref):
+    out_ref[...] = acc_ref[...] + products((swaps_ref[0], swaps_ref[1]), blocks_ref, 2)
+
+
+def gradient_kernel(group_size, blocks_ref, first_ref, second_ref, acc_ref,
                     query_ref, mixed_ref, inner_ref, flipped_ref,
                     conv_ref, qgrad_ref, sums_ref):
     rows, width = acc_ref.shape
-    mixed_grad = acc_ref[...] + products((first_ref[...], second_ref[...]), pair_ref)
+    mixed_grad = acc_ref[...] + products((first_ref[...], second_ref[...]), blocks_ref, 3)
     conv = (mixed_grad * query_ref[...].astype(F32)).astype(BF16)
     conv_ref[...] = conv
     qgrad_ref[...] = (mixed_grad * mixed_ref[...]).astype(BF16)
@@ -257,61 +242,47 @@
     inner = (key_act.astype(F32) * value_act.astype(F32)).astype(BF16)
 
     hbm = pl.BlockSpec(memory_space=pltpu.HBM)
-    pair = ((2, width, depth), BF16)
     wide = (rows, width)
-    sem = [pltpu.SemaphoreType.DMA((2 * PIECES,))]
 
     ring1 = ring(out_grad)
     swap0 = swap(out_grad)
     before = passed_along(inner, "ctx", 1)
     ring2 = ring(swap0)
-    fwd, bwd, pair0, pair1 = call(
-        stage_kernel,
-        [((groups, taps, 2 * taps), BF16)] * 2 + [pair] * 2,
-        (filters, out_weight),
-        8 * groups * taps * taps,
-        [hbm, hbm],
-        [pltpu.VMEM(filters.shape, BF16), pltpu.SemaphoreType.DMA] + sem * 2,
+    blocks = call(
+        load_kernel,
+        [((ch_size, width, depth), BF16)],
+        (out_weight,),
+        1 << 20,
+        [hbm],
+        [pltpu.SemaphoreType.DMA((ch_size,))],
         VMEM_MIB,
-    )
-    acc = call(
-        first_product_kernel,
-        [(wide, F32)],
-        (out_grad, swap0, pair0),
-        4 * rows * depth * width,
     )[0]
     ring3 = ring(ring1)
-    mixed, gated, flipped, packed, pair2 = call(
+    fwd, bwd = call(
+        tables_kernel, [((groups, taps, 2 * taps), BF16)] * 2, (filters,), 8 * groups * taps * taps
+    )
+    mixed, gated, flipped, packed = call(
         functools.partial(forward_kernel, group_size),
-        [(wide, F32), (wide, BF16), ((3 * rows - 16, width), BF16), ((2, rows, depth), BF16), pair],
-        (before, inner, query_act, skip_row, fwd, ring1, ring2, out_weight),
+        [(wide, F32), (wide, BF16), ((3 * rows - 16, width), BF16), ((2, rows, depth), BF16)],
+        (before, inner, query_act, skip_row, fwd, ring1, ring2),
         4 * rows * rows * width * 8,
-        [VMEM_SPEC] * 7 + [hbm],
-        sem,
-        VMEM_MIB,
     )
     swap12 = swap(packed)
-    acc, pair3 = call(
-        second_product_kernel,
-        [(wide, F32), pair],
-        (ring1, ring2, pair1, acc, out_weight),
-        4 * rows * depth * width,
-        [VMEM_SPEC] * 4 + [hbm],
-        sem,
-        VMEM_MIB,
-    )
+    acc = call(
+        first_product_kernel, [(wide, F32)], (out_grad, swap0, blocks), 4 * rows * depth * width
+    )[0]
+    acc = call(
+        second_product_kernel, [(wide, F32)], (ring1, ring2, blocks, acc), 4 * rows * depth * width
+    )[0]
     swap3 = swap(ring3)
     acc = call(
-        third_product_kernel,
-        [(wide, F32)],
-        (swap12, pair2, acc),
-        4 * rows * depth * width,
+        third_product_kernel, [(wide, F32)], (swap12, blocks, acc), 4 * rows * depth * width
     )[0]
     planes = ctx_size // Z_SIZE
     conv, query_grad, sums = call(
         functools.partial(gradient_kernel, group_size),
         [(wide, BF16), (wide, BF16), ((Z_SIZE, SUM_ROWS, LANES), F32)],
-        (pair3, ring3, swap3, acc, query_act, mixed, inner, flipped),
+        (blocks, ring3, swap3, acc, query_act, mixed, inner, flipped),
         8 * rows * depth * width,
     )
     along_z = [[p * Z_SIZE + z for z in range(Z_SIZE)] for p in range(planes)]

time: 101 us -> 103 us (1.020)
  waiting for transfers between devices: 16.3 us -> 17.9 us
  local copies, waits for them, and re-layouts: 0.72 us -> 2.31 us
    unnamed x12 -> x16, local copies, waits for them, and re-layouts: 0.72 us -> 2.31 us
    ppermute x2, waiting for transfers between devices: 5 us -> 6.43 us  [passed_along(): return lax.ppermute(block, axis, route)]
    pallas_call x9 -> x10, Pallas kernels: 14.2 us -> 13.3 us  [call(): pl.pallas_call(kernel, out_shape=[jax.ShapeDtypeStruct(s, d) for s, d in...]
where the time goes in v3:
time: 103 us; the launch traced here: 102 us
  starting transfers between devices  45 us (44%)
  blocking collectives  21.8 us (21%)
  waiting for transfers between devices  17.9 us (17%)
  Pallas kernels  13.3 us (13%)
  local copies, waits for them, and re-layouts  2.31 us (2%)
    ppermute x3, starting transfers between devices, swap(): return lax.ppermute(block, 'ch', [(c, c ^ 1) for c in range(ch_size)])  24.1 us
    all_to_all x1, blocking collectives, exchanged(): lax.all_to_all(blocks, 'ctx', 0, 0, axis_index_groups=groups, tiled=True)  21.8 us
    pallas_call x10, Pallas kernels, call(): pl.pallas_call(kernel, out_shape=[jax.ShapeDtypeStruct(s, d) for s, d in...  13.3 us
    all_to_all x1, starting transfers between devices, exchanged(): lax.all_to_all(blocks, 'ctx', 0, 0, axis_index_groups=groups, tiled=True)  11 us
    ppermute x3, starting transfers between devices, ring(): return lax.ppermute(block, 'ch', [(c, to(c)) for c in range(ch_size)])  7.3 us
    ppermute x3, waiting for transfers between devices, ring(): return lax.ppermute(block, 'ch', [(c, to(c)) for c in range(ch_size)])  6.9 us
    ppermute x2, waiting for transfers between devices, passed_along(): return lax.ppermute(block, axis, route)  6.43 us
    all_to_all x1, waiting for transfers between devices, exchanged(): lax.all_to_all(blocks, 'ctx', 0, 0, axis_index_groups=groups, tiled=True)  4.57 us
  transfers between devices with their start and end apart: 9, of which 5 were waited for; matrix products, arithmetic and copies ran while one was open for 1% of the time, Pallas kernels for 8%

profile of v3, /device:TPU:1, one launch (start us, length us, event | category | flops | bytes accessed | tf_op | source)
XLA Modules:
  0.0 102.1 jit_solution(13612620122014965893)
XLA Ops:
  0.6 16.0 %collective-permute-start.2 = (bf16[128,1024]{1,0:T(8,128)(2,1)}, bf16[128,1024]{1,0:T(8,128)(2,1)S(1)}, u32[]{:S(2)}, u32[]{:S(2)}) collective-permute-start(bf16[128,1024]{1,0:T(8,128)(2,1)} %own_ref.1), channel_id=1, source_target_pairs={{0,1},{1,0},{2,3},{3,2},{4,5},{5,4},{6,7},{7,6},{8,9},{9,8},{10,11... | collective-permute-start | bytes 786440 | tf_op jit(solution)/shard_map/ppermute | solution.py:239
  16.7 1.9 %collective-permute-start.1 = (bf16[128,1024]{1,0:T(8,128)(2,1)}, bf16[128,1024]{1,0:T(8,128)(2,1)S(1)}, u32[]{:S(2)}, u32[]{:S(2)}) collective-permute-start(bf16[128,1024]{1,0:T(8,128)(2,1)} %own_ref.1), channel_id=1, source_target_pairs={{0,2},{1,7},{2,4},{3,1},{4,6},{5,3},{6,0},{7,5},{8,10},{9,15},{10,... | collective-permute-start | bytes 786440 | tf_op jit(solution)/shard_map/ppermute | solution.py:236
  18.6 1.9 %collective-permute-start.3 = (bf16[128,1024]{1,0:T(8,128)(2,1)S(1)}, bf16[128,1024]{1,0:T(8,128)(2,1)S(1)}, u32[]{:S(2)}, u32[]{:S(2)}) collective-permute-start(bf16[128,1024]{1,0:T(8,128)(2,1)S(1)} %collective-permute-done.2.swap_ref), channel_id=1, source_target_pairs={{0,2},{1,7},{2,4},{3,1},{4,6},{5,3},{6,0},{7,5},{8,10},{9,15},{10,... | collective-permute-start | bytes 786440 | tf_op jit(solution)/shard_map/ppermute | solution.py:236
  20.5 1.0 multiply_convert_fusion.inner_ref
  21.5 1.3 %collective-permute-start = (bf16[128,512]{1,0:T(8,128)(2,1)S(1)}, bf16[128,512]{1,0:T(8,128)(2,1)S(1)}, u32[]{:S(2)}, u32[]{:S(2)}) collective-permute-start(bf16[128,512]{1,0:T(8,128)(2,1)S(1)} %multiply_convert_fusion.inner_ref), channel_id=1, source_target_pairs={{0,8},{8,16},{16,24},{24,32},{32,40},{40,48},{48,56},{56,64},{64,7... | collective-permute-start | bytes 393224 | tf_op jit(solution)/shard_map/ppermute | solution.py:218
  22.9 0.7 copy-done.7
  23.5 0.9 shard_map.118
  24.4 1.5 %collective-permute-done.before_ref = bf16[128,512]{1,0:T(8,128)(2,1)S(1)} collective-permute-done((bf16[128,512]{1,0:T(8,128)(2,1)S(1)}, bf16[128,512]{1,0:T(8,128)(2,1)S(1)}, u32[]{:S(2)}, u32[]{:S(2)}) %collective-permute-start) | collective-permute-done | bytes 131104 | tf_op jit(solution)/shard_map/ppermute | solution.py:218
  25.9 2.1 %collective-permute-done.3.ring2_ref = bf16[128,1024]{1,0:T(8,128)(2,1)S(1)} collective-permute-done((bf16[128,1024]{1,0:T(8,128)(2,1)S(1)}, bf16[128,1024]{1,0:T(8,128)(2,1)S(1)}, u32[]{:S(2)}, u32[]{:S(2)}) %collective-permute-start.3) | collective-permute-done | bytes 262176 | tf_op jit(solution)/shard_map/ppermute | solution.py:236
  28.0 0.9 copy-done
  28.9 0.7 copy-done.5
  29.6 1.4 %shard_map.119 = (f32[128,512]{1,0:T(8,128)S(1)}, bf16[128,512]{1,0:T(8,128)(2,1)}, bf16[368,512]{1,0:T(8,128)(2,1)S(1)}, bf16[2,128,1024]{2,1,0:T(8,128)(2,1)S(1)}) custom-call(bf16[128,512]{1,0:T(8,128)(2,1)S(1)} %collective-permute-done.before_ref, bf16[128,512]{1,0:T(8,128)(2,1)S(1)} %multiply_convert_fusion.inner_ref, bf16[128,512]{1,0:T(8,128)(2,1)S(1)} %copy-done, ...), custom_call_target="tpu_custom_call" | custom-call | flops 268435456 | bytes 4194304 | tf_op jit(solution)/shard_map/pallas_call | solution.py:204
  31.0 4.1 %collective-permute-start.6 = (bf16[2,128,1024]{2,1,0:T(8,128)(2,1)S(1)}, bf16[2,128,1024]{2,1,0:T(8,128)(2,1)S(1)}, u32[]{:S(2)}, u32[]{:S(2)}) collective-permute-start(bf16[2,128,1024]{2,1,0:T(8,128)(2,1)S(1)} %get-tuple-element.21), channel_id=1, source_target_pairs={{0,1},{1,0},{2,3},{3,2},{4,5},{5,4},{6,7},{7,6},{8,9},{9,8},{10,11... | collective-permute-start | bytes 1572872 | tf_op jit(solution)/shard_map/ppermute | solution.py:239
  35.1 3.5 %collective-permute-start.4 = (bf16[128,1024]{1,0:T(8,128)(2,1)S(1)}, bf16[128,1024]{1,0:T(8,128)(2,1)S(1)}, u32[]{:S(2)}, u32[]{:S(2)}) collective-permute-start(bf16[128,1024]{1,0:T(8,128)(2,1)S(1)} %collective-permute-done.1.ring1_ref), channel_id=1, source_target_pairs={{0,2},{1,7},{2,4},{3,1},{4,6},{5,3},{6,0},{7,5},{8,10},{9,15},{10,... | collective-permute-start | bytes 786440 | tf_op jit(solution)/shard_map/ppermute | solution.py:236
  38.6 4.8 %collective-permute-done.4.first_ref = bf16[128,1024]{1,0:T(8,128)(2,1)S(1)} collective-permute-done((bf16[128,1024]{1,0:T(8,128)(2,1)S(1)}, bf16[128,1024]{1,0:T(8,128)(2,1)S(1)}, u32[]{:S(2)}, u32[]{:S(2)}) %collective-permute-start.4) | collective-permute-done | bytes 262176 | tf_op jit(solution)/shard_map/ppermute | solution.py:236
  43.4 4.0 %collective-permute-start.5 = (bf16[128,1024]{1,0:T(8,128)(2,1)S(1)}, bf16[128,1024]{1,0:T(8,128)(2,1)S(1)}, u32[]{:S(2)}, u32[]{:S(2)}) collective-permute-start(bf16[128,1024]{1,0:T(8,128)(2,1)S(1)} %collective-permute-done.4.first_ref), channel_id=1, source_target_pairs={{0,1},{1,0},{2,3},{3,2},{4,5},{5,4},{6,7},{7,6},{8,9},{9,8},{10,11... | collective-permute-start | bytes 786440 | tf_op jit(solution)/shard_map/ppermute | solution.py:239
  47.4 3.5 %shard_map.120.blocks_ref = bf16[8,512,1024]{2,1,0:T(8,128)(2,1)S(1)} custom-call(bf16[512,8192]{1,0:T(8,128)(2,1)} %weight_hbm.1), custom_call_target="tpu_custom_call" | custom-call | flops 1048576 | bytes 4194304 | tf_op jit(solution)/shard_map/pallas_call | solution.py:204
  50.9 0.8 shard_map.121.acc_ref
  51.8 0.0 copy-start.1
  51.8 0.8 shard_map.122.acc_ref
  52.6 0.0 copy-start.3
  52.6 0.0 copy-start.6
  52.7 0.8 shard_map.123.acc_ref
  53.5 2.2 %shard_map.124 = (bf16[128,512]{1,0:T(8,128)(2,1)S(1)}, bf16[128,512]{1,0:T(8,128)(2,1)}, f32[8,40,128]{2,1,0:T(8,128)S(1)}) custom-call(bf16[8,512,1024]{2,1,0:T(8,128)(2,1)S(1)} %shard_map.120.blocks_ref, bf16[128,1024]{1,0:T(8,128)(2,1)S(1)} %collective-permute-done.4.first_ref, bf16[128,1024]{1,0:T(8,128)(2,1)S(1)} %collective-permute-done.5.second_ref, ...), custom_call_target="tpu_custom_call" | custom-call | flops 536870912 | bytes 4194304 | tf_op jit(solution)/shard_map/pallas_call | solution.py:204
  55.7 21.8 %all_to_all.10.got_ref = f32[8,40,128]{2,1,0:T(8,128)S(1)} all-to-all(f32[8,40,128]{2,1,0:T(8,128)S(1)} %get-tuple-element.29), channel_id=1, replica_groups={{0,8,16,24,32,40,48,56},{64,72,80,88,96,104,112,120},{128,136,144,152,1..., dimensions={0} | all-to-all | bytes 327680 | tf_op jit(solution)/shard_map/all_to_all | solution.py:222
  77.5 0.8 shard_map.126
  78.3 11.0 %all-to-all-start.1 = ((f32[16,40,128]{2,1,0:T(8,128)}), f32[16,40,128]{2,1,0:T(8,128)S(1)}, u32[]{:S(2)}, u32[]{:S(2)}) async-start(f32[16,40,128]{2,1,0:T(8,128)} %shard_map.126), calls=%async_computation.1 | async-start | bytes 655360 | tf_op jit(solution)/shard_map/all_to_all | solution.py:222
  89.3 1.3 %collective-permute-start.7 = (bf16[128,512]{1,0:T(8,128)(2,1)S(1)}, bf16[128,512]{1,0:T(8,128)(2,1)S(1)}, u32[]{:S(2)}, u32[]{:S(2)}) collective-permute-start(bf16[128,512]{1,0:T(8,128)(2,1)S(1)} %get-tuple-element.25.conv_ref), channel_id=1, source_target_pairs={{8,0},{16,8},{24,16},{32,24},{40,32},{48,40},{56,48},{64,56},{72,6... | collective-permute-start | bytes 393224 | tf_op jit(solution)/shard_map/ppermute | solution.py:218
  90.6 4.9 %collective-permute-done.7.after_ref = bf16[128,512]{1,0:T(8,128)(2,1)S(1)} collective-permute-done((bf16[128,512]{1,0:T(8,128)(2,1)S(1)}, bf16[128,512]{1,0:T(8,128)(2,1)S(1)}, u32[]{:S(2)}, u32[]{:S(2)}) %collective-permute-start.7) | collective-permute-done | bytes 131104 | tf_op jit(solution)/shard_map/ppermute | solution.py:218
  95.5 1.4 %shard_map.125 = (bf16[128,512]{1,0:T(8,128)(2,1)}, bf16[128,512]{1,0:T(8,128)(2,1)}) custom-call(bf16[128,512]{1,0:T(8,128)(2,1)S(1)} %get-tuple-element.25.conv_ref, bf16[128,512]{1,0:T(8,128)(2,1)S(1)} %collective-permute-done.7.after_ref, bf16[128,512]{1,0:T(8,128)(2,1)S(1)} %copy-done.3, bf16[128,512]{1,0:T(8,128)(2,1)S(1)} %copy-done.2, ...), custom_call_target="tpu_custom_call" | custom-call | flops 268435456 | bytes 4194304 | tf_op jit(solution)/shard_map/pallas_call | solution.py:204
  96.9 4.6 %all-to-all-done.1.got_ref = f32[16,40,128]{2,1,0:T(8,128)S(1)} async-done(((f32[16,40,128]{2,1,0:T(8,128)}), f32[16,40,128]{2,1,0:T(8,128)S(1)}, u32[]{:S(2)}, u32[]{:S(2)}) %all-to-all-start.1) | async-done | bytes 327712 | tf_op jit(solution)/shard_map/all_to_all | solution.py:222
  101.5 0.6 shard_map.127
  (14 shorter events, 0.0 us)
Async XLA Ops:
  0.6 18.0 %collective-permute-start.2 = (bf16[128,1024]{1,0:T(8,128)(2,1)}, bf16[128,1024]{1,0:T(8,128)(2,1)S(1)}, u32[]{:S(2)}, u32[]{:S(2)}) collective-permute-start(bf16[128,1024]{1,0:T(8,128)(2,1)} %own_ref.1), channel_id=1, source_target_pairs={{0,1},{1,0},{2,3},{3,2},{4,5},{5,4},{6,7},{7,6},{8,9},{9,8},{10,11... | collective-permute-start | bytes 786440 | tf_op jit(solution)/shard_map/ppermute | solution.py:239
  16.7 9.3 %collective-permute-start.1 = (bf16[128,1024]{1,0:T(8,128)(2,1)}, bf16[128,1024]{1,0:T(8,128)(2,1)S(1)}, u32[]{:S(2)}, u32[]{:S(2)}) collective-permute-start(bf16[128,1024]{1,0:T(8,128)(2,1)} %own_ref.1), channel_id=1, source_target_pairs={{0,2},{1,7},{2,4},{3,1},{4,6},{5,3},{6,0},{7,5},{8,10},{9,15},{10,... | collective-permute-start | bytes 786440 | tf_op jit(solution)/shard_map/ppermute | solution.py:236
  18.6 9.4 %collective-permute-start.3 = (bf16[128,1024]{1,0:T(8,128)(2,1)S(1)}, bf16[128,1024]{1,0:T(8,128)(2,1)S(1)}, u32[]{:S(2)}, u32[]{:S(2)}) collective-permute-start(bf16[128,1024]{1,0:T(8,128)(2,1)S(1)} %collective-permute-done.2.swap_ref), channel_id=1, source_target_pairs={{0,2},{1,7},{2,4},{3,1},{4,6},{5,3},{6,0},{7,5},{8,10},{9,15},{10,... | collective-permute-start | bytes 786440 | tf_op jit(solution)/shard_map/ppermute | solution.py:236
  21.5 4.4 %collective-permute-start = (bf16[128,512]{1,0:T(8,128)(2,1)S(1)}, bf16[128,512]{1,0:T(8,128)(2,1)S(1)}, u32[]{:S(2)}, u32[]{:S(2)}) collective-permute-start(bf16[128,512]{1,0:T(8,128)(2,1)S(1)} %multiply_convert_fusion.inner_ref), channel_id=1, source_target_pairs={{0,8},{8,16},{16,24},{24,32},{32,40},{40,48},{48,56},{56,64},{64,7... | collective-permute-start | bytes 393224 | tf_op jit(solution)/shard_map/ppermute | solution.py:218
  22.8 0.7 copy-start.7
  28.0 0.9 copy-start
  28.9 0.7 copy-start.5
  31.0 19.9 %copy-start.4 = (bf16[128,1024]{1,0:T(8,128)(2,1)S(1)}, bf16[128,1024]{1,0:T(8,128)(2,1)}, u32[]{:S(2)}) copy-start(bf16[128,1024]{1,0:T(8,128)(2,1)} %own_ref.1) | copy-start | bytes 786436
  31.0 21.7 %collective-permute-start.6 = (bf16[2,128,1024]{2,1,0:T(8,128)(2,1)S(1)}, bf16[2,128,1024]{2,1,0:T(8,128)(2,1)S(1)}, u32[]{:S(2)}, u32[]{:S(2)}) collective-permute-start(bf16[2,128,1024]{2,1,0:T(8,128)(2,1)S(1)} %get-tuple-element.21), channel_id=1, source_target_pairs={{0,1},{1,0},{2,3},{3,2},{4,5},{5,4},{6,7},{7,6},{8,9},{9,8},{10,11... | collective-permute-start | bytes 1572872 | tf_op jit(solution)/shard_map/ppermute | solution.py:239
  35.1 8.3 %collective-permute-start.4 = (bf16[128,1024]{1,0:T(8,128)(2,1)S(1)}, bf16[128,1024]{1,0:T(8,128)(2,1)S(1)}, u32[]{:S(2)}, u32[]{:S(2)}) collective-permute-start(bf16[128,1024]{1,0:T(8,128)(2,1)S(1)} %collective-permute-done.1.ring1_ref), channel_id=1, source_target_pairs={{0,2},{1,7},{2,4},{3,1},{4,6},{5,3},{6,0},{7,5},{8,10},{9,15},{10,... | collective-permute-start | bytes 786440 | tf_op jit(solution)/shard_map/ppermute | solution.py:236
  43.4 10.1 %collective-permute-start.5 = (bf16[128,1024]{1,0:T(8,128)(2,1)S(1)}, bf16[128,1024]{1,0:T(8,128)(2,1)S(1)}, u32[]{:S(2)}, u32[]{:S(2)}) collective-permute-start(bf16[128,1024]{1,0:T(8,128)(2,1)S(1)} %collective-permute-done.4.first_ref), channel_id=1, source_target_pairs={{0,1},{1,0},{2,3},{3,2},{4,5},{5,4},{6,7},{7,6},{8,9},{9,8},{10,11... | collective-permute-start | bytes 786440 | tf_op jit(solution)/shard_map/ppermute | solution.py:239
  51.8 1.7 %copy-start.1 = (bf16[128,512]{1,0:T(8,128)(2,1)S(1)}, bf16[128,512]{1,0:T(8,128)(2,1)}, u32[]{:S(2)}) copy-start(bf16[128,512]{1,0:T(8,128)(2,1)} %query_ref.3) | copy-start | bytes 393220
  52.6 42.9 %copy-start.2 = (bf16[128,512]{1,0:T(8,128)(2,1)S(1)}, bf16[128,512]{1,0:T(8,128)(2,1)}, u32[]{:S(2)}) copy-start(bf16[128,512]{1,0:T(8,128)(2,1)} %value_ref.1) | copy-start | bytes 393220
  52.6 42.8 %copy-start.3 = (bf16[128,512]{1,0:T(8,128)(2,1)S(1)}, bf16[128,512]{1,0:T(8,128)(2,1)}, u32[]{:S(2)}) copy-start(bf16[128,512]{1,0:T(8,128)(2,1)} %key_ref.1) | copy-start | bytes 393220
  52.6 42.8 %copy-start.6 = (f32[512]{0:T(512)S(1)}, f32[512]{0:T(512)}, u32[]{:S(2)}) copy-start(f32[512]{0:T(512)} %param.11) | copy-start | bytes 6148
  78.3 23.2 %all-to-all-start.1 = ((f32[16,40,128]{2,1,0:T(8,128)}), f32[16,40,128]{2,1,0:T(8,128)S(1)}, u32[]{:S(2)}, u32[]{:S(2)}) async-start(f32[16,40,128]{2,1,0:T(8,128)} %shard_map.126), calls=%async_computation.1 | async-start | bytes 655360 | tf_op jit(solution)/shard_map/all_to_all | solution.py:222
  89.3 6.2 %collective-permute-start.7 = (bf16[128,512]{1,0:T(8,128)(2,1)S(1)}, bf16[128,512]{1,0:T(8,128)(2,1)S(1)}, u32[]{:S(2)}, u32[]{:S(2)}) collective-permute-start(bf16[128,512]{1,0:T(8,128)(2,1)S(1)} %get-tuple-element.25.conv_ref), channel_id=1, source_target_pairs={{8,0},{16,8},{24,16},{32,24},{40,32},{48,40},{56,48},{64,56},{72,6... | collective-permute-start | bytes 393224 | tf_op jit(solution)/shard_map/ppermute | solution.py:218

commit v4 on v3

--- a/solution.py
+++ b/solution.py
@@ -11,7 +11,7 @@
 BF16 = jnp.bfloat16
 F32 = jnp.float32
 LANES = 128
-Z_SIZE = 8
+X_SIZE = 8
 CORES = 2
 SUM_ROWS = 40
 VMEM_MIB = 42
@@ -278,19 +278,19 @@
     acc = call(
         third_product_kernel, [(wide, F32)], (swap12, blocks, acc), 4 * rows * depth * width
     )[0]
-    planes = ctx_size // Z_SIZE
+    near = ctx_size // X_SIZE
     conv, query_grad, sums = call(
         functools.partial(gradient_kernel, group_size),
-        [(wide, BF16), (wide, BF16), ((Z_SIZE, SUM_ROWS, LANES), F32)],
+        [(wide, BF16), (wide, BF16), ((X_SIZE, SUM_ROWS, LANES), F32)],
         (blocks, ring3, swap3, acc, query_act, mixed, inner, flipped),
         8 * rows * depth * width,
     )
-    along_z = [[p * Z_SIZE + z for z in range(Z_SIZE)] for p in range(planes)]
-    across_z = [[p * Z_SIZE + z for p in range(planes)] for z in range(Z_SIZE)]
-    sums = exchanged(sums, along_z)
+    along_x = [[x * near + r for x in range(X_SIZE)] for r in range(near)]
+    same_x = [[x * near + r for r in range(near)] for x in range(X_SIZE)]
+    sums = exchanged(sums, along_x)
     after = passed_along(conv, "ctx", -1)
-    sums = call(fold_kernel, [((planes, SUM_ROWS, LANES), F32)], (sums,), 1 << 20)[0]
-    sums = exchanged(sums, across_z)
+    sums = call(fold_kernel, [((near, SUM_ROWS, LANES), F32)], (sums,), 1 << 20)[0]
+    sums = exchanged(sums, same_x)
     key_grad, value_grad = call(
         functools.partial(backward_kernel, group_size),
         [(wide, BF16)] * 2,

time: 103 us -> 102 us (level)
  starting transfers between devices: 45 us -> 37.9 us
  blocking collectives: 21.8 us -> 27.4 us
    all_to_all x1, starting transfers between devices: 11 us -> 3.9 us  [exchanged(): lax.all_to_all(blocks, 'ctx', 0, 0, axis_index_groups=groups, tiled=True)]
    all_to_all x1, blocking collectives: 21.8 us -> 27.4 us  [exchanged(): lax.all_to_all(blocks, 'ctx', 0, 0, axis_index_groups=groups, tiled=True)]
    ppermute x2, waiting for transfers between devices: 6.43 us -> 12 us  [passed_along(): return lax.ppermute(block, axis, route)]
    all_to_all x1, waiting for transfers between devices: 4.57 us -> 0.01 us  [exchanged(): lax.all_to_all(blocks, 'ctx', 0, 0, axis_index_groups=groups, tiled=True)]
  transfers between devices with their start and end apart: 9 -> 9, of which waited for: 5 -> 4; matrix products, arithmetic and copies ran while one was open for 1% -> 1% of each run, Pallas kernels for 8% -> 8%
where the time goes in v4:
time: 102 us
  starting transfers between devices  37.9 us (37%)
  blocking collectives  27.4 us (27%)
  waiting for transfers between devices  18.9 us (19%)
  Pallas kernels  13.3 us (13%)
  local copies, waits for them, and re-layouts  2.31 us (2%)
    all_to_all x1, blocking collectives, exchanged(): lax.all_to_all(blocks, 'ctx', 0, 0, axis_index_groups=groups, tiled=True)  27.4 us
    ppermute x3, starting transfers between devices, swap(): return lax.ppermute(block, 'ch', [(c, c ^ 1) for c in range(ch_size)])  24.1 us
    pallas_call x10, Pallas kernels, call(): pl.pallas_call(kernel, out_shape=[jax.ShapeDtypeStruct(s, d) for s, d in...  13.3 us
    ppermute x2, waiting for transfers between devices, passed_along(): return lax.ppermute(block, axis, route)  12 us
    ppermute x3, starting transfers between devices, ring(): return lax.ppermute(block, 'ch', [(c, to(c)) for c in range(ch_size)])  7.3 us
    ppermute x3, waiting for transfers between devices, ring(): return lax.ppermute(block, 'ch', [(c, to(c)) for c in range(ch_size)])  6.9 us
    all_to_all x1, starting transfers between devices, exchanged(): lax.all_to_all(blocks, 'ctx', 0, 0, axis_index_groups=groups, tiled=True)  3.9 us
    ppermute x2, starting transfers between devices, passed_along(): return lax.ppermute(block, axis, route)  2.59 us
  transfers between devices with their start and end apart: 9, of which 4 were waited for; matrix products, arithmetic and copies ran while one was open for 1% of the time, Pallas kernels for 8%

profile of v4, /device:TPU:1, one launch (start us, length us, event | category | flops | bytes accessed | tf_op | source)
XLA Modules:
  0.0 101.6 jit_solution(11564884727685129237)
XLA Ops:
  0.6 16.0 %collective-permute-start.2 = (bf16[128,1024]{1,0:T(8,128)(2,1)}, bf16[128,1024]{1,0:T(8,128)(2,1)S(1)}, u32[]{:S(2)}, u32[]{:S(2)}) collective-permute-start(bf16[128,1024]{1,0:T(8,128)(2,1)} %own_ref.1), channel_id=1, source_target_pairs={{0,1},{1,0},{2,3},{3,2},{4,5},{5,4},{6,7},{7,6},{8,9},{9,8},{10,11... | collective-permute-start | bytes 786440 | tf_op jit(solution)/shard_map/ppermute | solution.py:239
  16.7 1.9 %collective-permute-start.1 = (bf16[128,1024]{1,0:T(8,128)(2,1)}, bf16[128,1024]{1,0:T(8,128)(2,1)S(1)}, u32[]{:S(2)}, u32[]{:S(2)}) collective-permute-start(bf16[128,1024]{1,0:T(8,128)(2,1)} %own_ref.1), channel_id=1, source_target_pairs={{0,2},{1,7},{2,4},{3,1},{4,6},{5,3},{6,0},{7,5},{8,10},{9,15},{10,... | collective-permute-start | bytes 786440 | tf_op jit(solution)/shard_map/ppermute | solution.py:236
  18.6 1.9 %collective-permute-start.3 = (bf16[128,1024]{1,0:T(8,128)(2,1)S(1)}, bf16[128,1024]{1,0:T(8,128)(2,1)S(1)}, u32[]{:S(2)}, u32[]{:S(2)}) collective-permute-start(bf16[128,1024]{1,0:T(8,128)(2,1)S(1)} %collective-permute-done.2.swap_ref), channel_id=1, source_target_pairs={{0,2},{1,7},{2,4},{3,1},{4,6},{5,3},{6,0},{7,5},{8,10},{9,15},{10,... | collective-permute-start | bytes 786440 | tf_op jit(solution)/shard_map/ppermute | solution.py:236
  20.5 1.0 multiply_convert_fusion.inner_ref
  21.5 1.3 %collective-permute-start = (bf16[128,512]{1,0:T(8,128)(2,1)S(1)}, bf16[128,512]{1,0:T(8,128)(2,1)S(1)}, u32[]{:S(2)}, u32[]{:S(2)}) collective-permute-start(bf16[128,512]{1,0:T(8,128)(2,1)S(1)} %multiply_convert_fusion.inner_ref), channel_id=1, source_target_pairs={{0,8},{8,16},{16,24},{24,32},{32,40},{40,48},{48,56},{56,64},{64,7... | collective-permute-start | bytes 393224 | tf_op jit(solution)/shard_map/ppermute | solution.py:218
  22.8 0.0 copy-start.7
  22.9 0.7 copy-done.7
  23.5 0.9 shard_map.118
  24.4 1.5 %collective-permute-done.before_ref = bf16[128,512]{1,0:T(8,128)(2,1)S(1)} collective-permute-done((bf16[128,512]{1,0:T(8,128)(2,1)S(1)}, bf16[128,512]{1,0:T(8,128)(2,1)S(1)}, u32[]{:S(2)}, u32[]{:S(2)}) %collective-permute-start) | collective-permute-done | bytes 131104 | tf_op jit(solution)/shard_map/ppermute | solution.py:218
  25.9 2.1 %collective-permute-done.3.ring2_ref = bf16[128,1024]{1,0:T(8,128)(2,1)S(1)} collective-permute-done((bf16[128,1024]{1,0:T(8,128)(2,1)S(1)}, bf16[128,1024]{1,0:T(8,128)(2,1)S(1)}, u32[]{:S(2)}, u32[]{:S(2)}) %collective-permute-start.3) | collective-permute-done | bytes 262176 | tf_op jit(solution)/shard_map/ppermute | solution.py:236
  28.0 0.9 copy-done
  28.9 0.7 copy-done.5
  29.6 1.4 %shard_map.119 = (f32[128,512]{1,0:T(8,128)S(1)}, bf16[128,512]{1,0:T(8,128)(2,1)}, bf16[368,512]{1,0:T(8,128)(2,1)S(1)}, bf16[2,128,1024]{2,1,0:T(8,128)(2,1)S(1)}) custom-call(bf16[128,512]{1,0:T(8,128)(2,1)S(1)} %collective-permute-done.before_ref, bf16[128,512]{1,0:T(8,128)(2,1)S(1)} %multiply_convert_fusion.inner_ref, bf16[128,512]{1,0:T(8,128)(2,1)S(1)} %copy-done, ...), custom_call_target="tpu_custom_call" | custom-call | flops 268435456 | bytes 4194304 | tf_op jit(solution)/shard_map/pallas_call | solution.py:204
  31.0 4.1 %collective-permute-start.6 = (bf16[2,128,1024]{2,1,0:T(8,128)(2,1)S(1)}, bf16[2,128,1024]{2,1,0:T(8,128)(2,1)S(1)}, u32[]{:S(2)}, u32[]{:S(2)}) collective-permute-start(bf16[2,128,1024]{2,1,0:T(8,128)(2,1)S(1)} %get-tuple-element.21), channel_id=1, source_target_pairs={{0,1},{1,0},{2,3},{3,2},{4,5},{5,4},{6,7},{7,6},{8,9},{9,8},{10,11... | collective-permute-start | bytes 1572872 | tf_op jit(solution)/shard_map/ppermute | solution.py:239
  35.1 3.5 %collective-permute-start.4 = (bf16[128,1024]{1,0:T(8,128)(2,1)S(1)}, bf16[128,1024]{1,0:T(8,128)(2,1)S(1)}, u32[]{:S(2)}, u32[]{:S(2)}) collective-permute-start(bf16[128,1024]{1,0:T(8,128)(2,1)S(1)} %collective-permute-done.1.ring1_ref), channel_id=1, source_target_pairs={{0,2},{1,7},{2,4},{3,1},{4,6},{5,3},{6,0},{7,5},{8,10},{9,15},{10,... | collective-permute-start | bytes 786440 | tf_op jit(solution)/shard_map/ppermute | solution.py:236
  38.6 4.8 %collective-permute-done.4.first_ref = bf16[128,1024]{1,0:T(8,128)(2,1)S(1)} collective-permute-done((bf16[128,1024]{1,0:T(8,128)(2,1)S(1)}, bf16[128,1024]{1,0:T(8,128)(2,1)S(1)}, u32[]{:S(2)}, u32[]{:S(2)}) %collective-permute-start.4) | collective-permute-done | bytes 262176 | tf_op jit(solution)/shard_map/ppermute | solution.py:236
  43.4 4.0 %collective-permute-start.5 = (bf16[128,1024]{1,0:T(8,128)(2,1)S(1)}, bf16[128,1024]{1,0:T(8,128)(2,1)S(1)}, u32[]{:S(2)}, u32[]{:S(2)}) collective-permute-start(bf16[128,1024]{1,0:T(8,128)(2,1)S(1)} %collective-permute-done.4.first_ref), channel_id=1, source_target_pairs={{0,1},{1,0},{2,3},{3,2},{4,5},{5,4},{6,7},{7,6},{8,9},{9,8},{10,11... | collective-permute-start | bytes 786440 | tf_op jit(solution)/shard_map/ppermute | solution.py:239
  47.4 3.5 %shard_map.120.blocks_ref = bf16[8,512,1024]{2,1,0:T(8,128)(2,1)S(1)} custom-call(bf16[512,8192]{1,0:T(8,128)(2,1)} %weight_hbm.1), custom_call_target="tpu_custom_call" | custom-call | flops 1048576 | bytes 4194304 | tf_op jit(solution)/shard_map/pallas_call | solution.py:204
  50.9 0.8 shard_map.121.acc_ref
  51.8 0.0 copy-start.1
  51.8 0.8 shard_map.122.acc_ref
  52.6 0.0 copy-start.3
  52.6 0.0 copy-start.6
  52.7 0.8 shard_map.123.acc_ref
  53.5 2.2 %shard_map.124 = (bf16[128,512]{1,0:T(8,128)(2,1)S(1)}, bf16[128,512]{1,0:T(8,128)(2,1)}, f32[8,40,128]{2,1,0:T(8,128)S(1)}) custom-call(bf16[8,512,1024]{2,1,0:T(8,128)(2,1)S(1)} %shard_map.120.blocks_ref, bf16[128,1024]{1,0:T(8,128)(2,1)S(1)} %collective-permute-done.4.first_ref, bf16[128,1024]{1,0:T(8,128)(2,1)S(1)} %collective-permute-done.5.second_ref, ...), custom_call_target="tpu_custom_call" | custom-call | flops 536870912 | bytes 4194304 | tf_op jit(solution)/shard_map/pallas_call | solution.py:204
  55.7 27.4 %all_to_all.10.got_ref = f32[8,40,128]{2,1,0:T(8,128)S(1)} all-to-all(f32[8,40,128]{2,1,0:T(8,128)S(1)} %get-tuple-element.29), channel_id=1, replica_groups={{0,128,256,384,512,640,768,896},{8,136,264,392,520,648,776,904},{16,144..., dimensions={0} | all-to-all | bytes 327680 | tf_op jit(solution)/shard_map/all_to_all | solution.py:222
  83.1 0.8 shard_map.126
  83.9 3.9 %all-to-all-start.1 = ((f32[16,40,128]{2,1,0:T(8,128)}), f32[16,40,128]{2,1,0:T(8,128)S(1)}, u32[]{:S(2)}, u32[]{:S(2)}) async-start(f32[16,40,128]{2,1,0:T(8,128)} %shard_map.126), calls=%async_computation.1 | async-start | bytes 655360 | tf_op jit(solution)/shard_map/all_to_all | solution.py:222
  87.8 1.3 %collective-permute-start.7 = (bf16[128,512]{1,0:T(8,128)(2,1)S(1)}, bf16[128,512]{1,0:T(8,128)(2,1)S(1)}, u32[]{:S(2)}, u32[]{:S(2)}) collective-permute-start(bf16[128,512]{1,0:T(8,128)(2,1)S(1)} %get-tuple-element.25.conv_ref), channel_id=1, source_target_pairs={{8,0},{16,8},{24,16},{32,24},{40,32},{48,40},{56,48},{64,56},{72,6... | collective-permute-start | bytes 393224 | tf_op jit(solution)/shard_map/ppermute | solution.py:218
  89.1 10.4 %collective-permute-done.7.after_ref = bf16[128,512]{1,0:T(8,128)(2,1)S(1)} collective-permute-done((bf16[128,512]{1,0:T(8,128)(2,1)S(1)}, bf16[128,512]{1,0:T(8,128)(2,1)S(1)}, u32[]{:S(2)}, u32[]{:S(2)}) %collective-permute-start.7) | collective-permute-done | bytes 131104 | tf_op jit(solution)/shard_map/ppermute | solution.py:218
  99.5 1.4 %shard_map.125 = (bf16[128,512]{1,0:T(8,128)(2,1)}, bf16[128,512]{1,0:T(8,128)(2,1)}) custom-call(bf16[128,512]{1,0:T(8,128)(2,1)S(1)} %get-tuple-element.25.conv_ref, bf16[128,512]{1,0:T(8,128)(2,1)S(1)} %collective-permute-done.7.after_ref, bf16[128,512]{1,0:T(8,128)(2,1)S(1)} %copy-done.3, bf16[128,512]{1,0:T(8,128)(2,1)S(1)} %copy-done.2, ...), custom_call_target="tpu_custom_call" | custom-call | flops 268435456 | bytes 4194304 | tf_op jit(solution)/shard_map/pallas_call | solution.py:204
  101.0 0.6 shard_map.127
  (14 shorter events, 0.0 us)
Async XLA Ops:
  0.6 18.0 %collective-permute-start.2 = (bf16[128,1024]{1,0:T(8,128)(2,1)}, bf16[128,1024]{1,0:T(8,128)(2,1)S(1)}, u32[]{:S(2)}, u32[]{:S(2)}) collective-permute-start(bf16[128,1024]{1,0:T(8,128)(2,1)} %own_ref.1), channel_id=1, source_target_pairs={{0,1},{1,0},{2,3},{3,2},{4,5},{5,4},{6,7},{7,6},{8,9},{9,8},{10,11... | collective-permute-start | bytes 786440 | tf_op jit(solution)/shard_map/ppermute | solution.py:239
  16.7 9.3 %collective-permute-start.1 = (bf16[128,1024]{1,0:T(8,128)(2,1)}, bf16[128,1024]{1,0:T(8,128)(2,1)S(1)}, u32[]{:S(2)}, u32[]{:S(2)}) collective-permute-start(bf16[128,1024]{1,0:T(8,128)(2,1)} %own_ref.1), channel_id=1, source_target_pairs={{0,2},{1,7},{2,4},{3,1},{4,6},{5,3},{6,0},{7,5},{8,10},{9,15},{10,... | collective-permute-start | bytes 786440 | tf_op jit(solution)/shard_map/ppermute | solution.py:236
  18.6 9.4 %collective-permute-start.3 = (bf16[128,1024]{1,0:T(8,128)(2,1)S(1)}, bf16[128,1024]{1,0:T(8,128)(2,1)S(1)}, u32[]{:S(2)}, u32[]{:S(2)}) collective-permute-start(bf16[128,1024]{1,0:T(8,128)(2,1)S(1)} %collective-permute-done.2.swap_ref), channel_id=1, source_target_pairs={{0,2},{1,7},{2,4},{3,1},{4,6},{5,3},{6,0},{7,5},{8,10},{9,15},{10,... | collective-permute-start | bytes 786440 | tf_op jit(solution)/shard_map/ppermute | solution.py:236
  21.5 4.4 %collective-permute-start = (bf16[128,512]{1,0:T(8,128)(2,1)S(1)}, bf16[128,512]{1,0:T(8,128)(2,1)S(1)}, u32[]{:S(2)}, u32[]{:S(2)}) collective-permute-start(bf16[128,512]{1,0:T(8,128)(2,1)S(1)} %multiply_convert_fusion.inner_ref), channel_id=1, source_target_pairs={{0,8},{8,16},{16,24},{24,32},{32,40},{40,48},{48,56},{56,64},{64,7... | collective-permute-start | bytes 393224 | tf_op jit(solution)/shard_map/ppermute | solution.py:218
  22.8 0.7 copy-start.7
  28.0 0.9 copy-start
  28.9 0.7 copy-start.5
  31.0 19.9 %copy-start.4 = (bf16[128,1024]{1,0:T(8,128)(2,1)S(1)}, bf16[128,1024]{1,0:T(8,128)(2,1)}, u32[]{:S(2)}) copy-start(bf16[128,1024]{1,0:T(8,128)(2,1)} %own_ref.1) | copy-start | bytes 786436
  31.0 21.7 %collective-permute-start.6 = (bf16[2,128,1024]{2,1,0:T(8,128)(2,1)S(1)}, bf16[2,128,1024]{2,1,0:T(8,128)(2,1)S(1)}, u32[]{:S(2)}, u32[]{:S(2)}) collective-permute-start(bf16[2,128,1024]{2,1,0:T(8,128)(2,1)S(1)} %get-tuple-element.21), channel_id=1, source_target_pairs={{0,1},{1,0},{2,3},{3,2},{4,5},{5,4},{6,7},{7,6},{8,9},{9,8},{10,11... | collective-permute-start | bytes 1572872 | tf_op jit(solution)/shard_map/ppermute | solution.py:239
  35.1 8.3 %collective-permute-start.4 = (bf16[128,1024]{1,0:T(8,128)(2,1)S(1)}, bf16[128,1024]{1,0:T(8,128)(2,1)S(1)}, u32[]{:S(2)}, u32[]{:S(2)}) collective-permute-start(bf16[128,1024]{1,0:T(8,128)(2,1)S(1)} %collective-permute-done.1.ring1_ref), channel_id=1, source_target_pairs={{0,2},{1,7},{2,4},{3,1},{4,6},{5,3},{6,0},{7,5},{8,10},{9,15},{10,... | collective-permute-start | bytes 786440 | tf_op jit(solution)/shard_map/ppermute | solution.py:236
  43.4 10.1 %collective-permute-start.5 = (bf16[128,1024]{1,0:T(8,128)(2,1)S(1)}, bf16[128,1024]{1,0:T(8,128)(2,1)S(1)}, u32[]{:S(2)}, u32[]{:S(2)}) collective-permute-start(bf16[128,1024]{1,0:T(8,128)(2,1)S(1)} %collective-permute-done.4.first_ref), channel_id=1, source_target_pairs={{0,1},{1,0},{2,3},{3,2},{4,5},{5,4},{6,7},{7,6},{8,9},{9,8},{10,11... | collective-permute-start | bytes 786440 | tf_op jit(solution)/shard_map/ppermute | solution.py:239
  51.8 1.7 %copy-start.1 = (bf16[128,512]{1,0:T(8,128)(2,1)S(1)}, bf16[128,512]{1,0:T(8,128)(2,1)}, u32[]{:S(2)}) copy-start(bf16[128,512]{1,0:T(8,128)(2,1)} %query_ref.3) | copy-start | bytes 393220
  52.6 46.9 %copy-start.2 = (bf16[128,512]{1,0:T(8,128)(2,1)S(1)}, bf16[128,512]{1,0:T(8,128)(2,1)}, u32[]{:S(2)}) copy-start(bf16[128,512]{1,0:T(8,128)(2,1)} %value_ref.1) | copy-start | bytes 393220
  52.6 46.9 %copy-start.3 = (bf16[128,512]{1,0:T(8,128)(2,1)S(1)}, bf16[128,512]{1,0:T(8,128)(2,1)}, u32[]{:S(2)}) copy-start(bf16[128,512]{1,0:T(8,128)(2,1)} %key_ref.1) | copy-start | bytes 393220
  52.6 46.9 %copy-start.6 = (f32[512]{0:T(512)S(1)}, f32[512]{0:T(512)}, u32[]{:S(2)}) copy-start(f32[512]{0:T(512)} %param.11) | copy-start | bytes 6148
  83.9 17.1 %all-to-all-start.1 = ((f32[16,40,128]{2,1,0:T(8,128)}), f32[16,40,128]{2,1,0:T(8,128)S(1)}, u32[]{:S(2)}, u32[]{:S(2)}) async-start(f32[16,40,128]{2,1,0:T(8,128)} %shard_map.126), calls=%async_computation.1 | async-start | bytes 655360 | tf_op jit(solution)/shard_map/all_to_all | solution.py:222
  87.8 11.7 %collective-permute-start.7 = (bf16[128,512]{1,0:T(8,128)(2,1)S(1)}, bf16[128,512]{1,0:T(8,128)(2,1)S(1)}, u32[]{:S(2)}, u32[]{:S(2)}) collective-permute-start(bf16[128,512]{1,0:T(8,128)(2,1)S(1)} %get-tuple-element.25.conv_ref), channel_id=1, source_target_pairs={{8,0},{16,8},{24,16},{32,24},{40,32},{48,40},{56,48},{64,56},{72,6... | collective-permute-start | bytes 393224 | tf_op jit(solution)/shard_map/ppermute | solution.py:218

commit v5 on v4

--- a/solution.py
+++ b/solution.py
@@ -11,9 +11,10 @@
 BF16 = jnp.bfloat16
 F32 = jnp.float32
 LANES = 128
-X_SIZE = 8
+Z_SIZE = 8
+Y_LOW = 2
 CORES = 2
-SUM_ROWS = 40
+HALF_ROWS = 24
 VMEM_MIB = 42
 PAIR_DISTANCE = (0, -1, 1, 2)
 SWAPPED_PAIR = 2
@@ -169,11 +170,16 @@
                 total[g * sub : (g + 1) * sub], 1, axis=1, stride=1, stride_axis=0
             )
             found.append(jnp.sum(skewed[:, rows:], axis=0, keepdims=True))
-    found += [skip[:, i * LANES : (i + 1) * LANES] for i in range(width // LANES)]
-    found.append(jnp.zeros((sums_ref.shape[1] - len(found), LANES), F32))
-    sums = jnp.concatenate(found, axis=0)
+    found_skip = [skip[:, i * LANES : (i + 1) * LANES] for i in range(width // LANES)]
+    filt_rows, skip_rows = len(found) // Y_LOW, len(found_skip) // Y_LOW
+    zeros = jnp.zeros((HALF_ROWS - filt_rows - skip_rows, LANES), F32)
+    halves = []
+    for y in range(Y_LOW):
+        filt_part = found[y * filt_rows : (y + 1) * filt_rows]
+        skip_part = found_skip[y * skip_rows : (y + 1) * skip_rows]
+        halves.append(jnp.concatenate(filt_part + skip_part + [zeros], axis=0))
     for i in range(sums_ref.shape[0]):
-        sums_ref[i] = sums
+        sums_ref[i] = halves[i % Y_LOW]
 
 
 def fold_kernel(got_ref, out_ref):
@@ -183,11 +189,15 @@
 
 
 def finish_kernel(got_ref, filter_ref, skip_ref):
-    total = jnp.sum(got_ref[...], axis=0)
-    groups = filter_ref.shape[0]
-    filter_ref[...] = total[:groups]
-    for i in range(skip_ref.shape[1] // LANES):
-        skip_ref[:, i * LANES : (i + 1) * LANES] = total[groups + i : groups + i + 1]
+    along_z = got_ref.shape[0] // Y_LOW
+    filt_rows = filter_ref.shape[0] // Y_LOW
+    skip_rows = skip_ref.shape[1] // LANES // Y_LOW
+    for y in range(Y_LOW):
+        total = jnp.sum(got_ref[y * along_z : (y + 1) * along_z], axis=0)
+        filter_ref[y * filt_rows : (y + 1) * filt_rows] = total[:filt_rows]
+        for i in range(skip_rows):
+            at = (y * skip_rows + i) * LANES
+            skip_ref[:, at : at + LANES] = total[filt_rows + i : filt_rows + i + 1]
 
 
 def backward_kernel(group_size, conv_ref, after_ref, key_ref, value_ref, skip_ref, bwd_ref,
@@ -278,18 +288,18 @@
     acc = call(
         third_product_kernel, [(wide, F32)], (swap12, blocks, acc), 4 * rows * depth * width
     )[0]
-    near = ctx_size // X_SIZE
+    planes, near = ctx_size // Z_SIZE, Y_LOW * Z_SIZE
     conv, query_grad, sums = call(
         functools.partial(gradient_kernel, group_size),
-        [(wide, BF16), (wide, BF16), ((X_SIZE, SUM_ROWS, LANES), F32)],
+        [(wide, BF16), (wide, BF16), ((planes, HALF_ROWS, LANES), F32)],
         (blocks, ring3, swap3, acc, query_act, mixed, inner, flipped),
         8 * rows * depth * width,
     )
-    along_x = [[x * near + r for x in range(X_SIZE)] for r in range(near)]
-    same_x = [[x * near + r for r in range(near)] for x in range(X_SIZE)]
-    sums = exchanged(sums, along_x)
+    same_z = [[p * Z_SIZE + z for p in range(planes)] for z in range(Z_SIZE)]
+    same_x = [[x * near + r for r in range(near)] for x in range(planes // Y_LOW)]
+    sums = exchanged(sums, same_z)
     after = passed_along(conv, "ctx", -1)
-    sums = call(fold_kernel, [((near, SUM_ROWS, LANES), F32)], (sums,), 1 << 20)[0]
+    sums = call(fold_kernel, [((near, HALF_ROWS, LANES), F32)], (sums,), 1 << 20)[0]
     sums = exchanged(sums, same_x)
     key_grad, value_grad = call(
         functools.partial(backward_kernel, group_size),

time: 102 us -> 102 us (level)
  blocking collectives: 27.4 us -> 30.1 us
  waiting for transfers between devices: 18.9 us -> 16.9 us
    all_to_all x1, blocking collectives: 27.4 us -> 30.1 us  [exchanged(): lax.all_to_all(blocks, 'ctx', 0, 0, axis_index_groups=groups, tiled=True)]
    ppermute x2, waiting for transfers between devices: 12 us -> 10 us  [passed_along(): return lax.ppermute(block, axis, route)]
where the time goes in v5:
time: 102 us
  starting transfers between devices  37.5 us (37%)
  blocking collectives  30.1 us (30%)
  waiting for transfers between devices  16.9 us (17%)
  Pallas kernels  13.2 us (13%)
  local copies, waits for them, and re-layouts  2.31 us (2%)
    all_to_all x1, blocking collectives, exchanged(): lax.all_to_all(blocks, 'ctx', 0, 0, axis_index_groups=groups, tiled=True)  30.1 us
    ppermute x3, starting transfers between devices, swap(): return lax.ppermute(block, 'ch', [(c, c ^ 1) for c in range(ch_size)])  24.1 us
    pallas_call x10, Pallas kernels, call(): pl.pallas_call(kernel, out_shape=[jax.ShapeDtypeStruct(s, d) for s, d in...  13.2 us
    ppermute x2, waiting for transfers between devices, passed_along(): return lax.ppermute(block, axis, route)  10 us
    ppermute x3, starting transfers between devices, ring(): return lax.ppermute(block, 'ch', [(c, to(c)) for c in range(ch_size)])  7.3 us
    ppermute x3, waiting for transfers between devices, ring(): return lax.ppermute(block, 'ch', [(c, to(c)) for c in range(ch_size)])  6.9 us
    all_to_all x1, starting transfers between devices, exchanged(): lax.all_to_all(blocks, 'ctx', 0, 0, axis_index_groups=groups, tiled=True)  3.52 us
    ppermute x2, starting transfers between devices, passed_along(): return lax.ppermute(block, axis, route)  2.59 us
  transfers between devices with their start and end apart: 9, of which 4 were waited for; matrix products, arithmetic and copies ran while one was open for 1% of the time, Pallas kernels for 8%

profile of v5, /device:TPU:1, one launch (start us, length us, event | category | flops | bytes accessed | tf_op | source)
XLA Modules:
  0.0 101.9 jit_solution(8296983955500522338)
XLA Ops:
  0.6 16.0 %collective-permute-start.2 = (bf16[128,1024]{1,0:T(8,128)(2,1)}, bf16[128,1024]{1,0:T(8,128)(2,1)S(1)}, u32[]{:S(2)}, u32[]{:S(2)}) collective-permute-start(bf16[128,1024]{1,0:T(8,128)(2,1)} %own_ref.1), channel_id=1, source_target_pairs={{0,1},{1,0},{2,3},{3,2},{4,5},{5,4},{6,7},{7,6},{8,9},{9,8},{10,11... | collective-permute-start | bytes 786440 | tf_op jit(solution)/shard_map/ppermute | solution.py:249
  16.7 1.9 %collective-permute-start.1 = (bf16[128,1024]{1,0:T(8,128)(2,1)}, bf16[128,1024]{1,0:T(8,128)(2,1)S(1)}, u32[]{:S(2)}, u32[]{:S(2)}) collective-permute-start(bf16[128,1024]{1,0:T(8,128)(2,1)} %own_ref.1), channel_id=1, source_target_pairs={{0,2},{1,7},{2,4},{3,1},{4,6},{5,3},{6,0},{7,5},{8,10},{9,15},{10,... | collective-permute-start | bytes 786440 | tf_op jit(solution)/shard_map/ppermute | solution.py:246
  18.6 1.9 %collective-permute-start.3 = (bf16[128,1024]{1,0:T(8,128)(2,1)S(1)}, bf16[128,1024]{1,0:T(8,128)(2,1)S(1)}, u32[]{:S(2)}, u32[]{:S(2)}) collective-permute-start(bf16[128,1024]{1,0:T(8,128)(2,1)S(1)} %collective-permute-done.2.swap_ref), channel_id=1, source_target_pairs={{0,2},{1,7},{2,4},{3,1},{4,6},{5,3},{6,0},{7,5},{8,10},{9,15},{10,... | collective-permute-start | bytes 786440 | tf_op jit(solution)/shard_map/ppermute | solution.py:246
  20.5 1.0 multiply_convert_fusion.inner_ref
  21.5 1.3 %collective-permute-start = (bf16[128,512]{1,0:T(8,128)(2,1)S(1)}, bf16[128,512]{1,0:T(8,128)(2,1)S(1)}, u32[]{:S(2)}, u32[]{:S(2)}) collective-permute-start(bf16[128,512]{1,0:T(8,128)(2,1)S(1)} %multiply_convert_fusion.inner_ref), channel_id=1, source_target_pairs={{0,8},{8,16},{16,24},{24,32},{32,40},{40,48},{48,56},{56,64},{64,7... | collective-permute-start | bytes 393224 | tf_op jit(solution)/shard_map/ppermute | solution.py:228
  22.8 0.0 copy-start.7
  22.9 0.7 copy-done.7
  23.5 0.9 shard_map.118
  24.4 1.5 %collective-permute-done.before_ref = bf16[128,512]{1,0:T(8,128)(2,1)S(1)} collective-permute-done((bf16[128,512]{1,0:T(8,128)(2,1)S(1)}, bf16[128,512]{1,0:T(8,128)(2,1)S(1)}, u32[]{:S(2)}, u32[]{:S(2)}) %collective-permute-start) | collective-permute-done | bytes 131104 | tf_op jit(solution)/shard_map/ppermute | solution.py:228
  25.9 2.1 %collective-permute-done.3.ring2_ref = bf16[128,1024]{1,0:T(8,128)(2,1)S(1)} collective-permute-done((bf16[128,1024]{1,0:T(8,128)(2,1)S(1)}, bf16[128,1024]{1,0:T(8,128)(2,1)S(1)}, u32[]{:S(2)}, u32[]{:S(2)}) %collective-permute-start.3) | collective-permute-done | bytes 262176 | tf_op jit(solution)/shard_map/ppermute | solution.py:246
  28.0 0.9 copy-done
  28.9 0.7 copy-done.5
  29.6 1.4 %shard_map.119 = (f32[128,512]{1,0:T(8,128)S(1)}, bf16[128,512]{1,0:T(8,128)(2,1)}, bf16[368,512]{1,0:T(8,128)(2,1)S(1)}, bf16[2,128,1024]{2,1,0:T(8,128)(2,1)S(1)}) custom-call(bf16[128,512]{1,0:T(8,128)(2,1)S(1)} %collective-permute-done.before_ref, bf16[128,512]{1,0:T(8,128)(2,1)S(1)} %multiply_convert_fusion.inner_ref, bf16[128,512]{1,0:T(8,128)(2,1)S(1)} %copy-done, ...), custom_call_target="tpu_custom_call" | custom-call | flops 268435456 | bytes 4194304 | tf_op jit(solution)/shard_map/pallas_call | solution.py:214
  31.0 4.1 %collective-permute-start.6 = (bf16[2,128,1024]{2,1,0:T(8,128)(2,1)S(1)}, bf16[2,128,1024]{2,1,0:T(8,128)(2,1)S(1)}, u32[]{:S(2)}, u32[]{:S(2)}) collective-permute-start(bf16[2,128,1024]{2,1,0:T(8,128)(2,1)S(1)} %get-tuple-element.21), channel_id=1, source_target_pairs={{0,1},{1,0},{2,3},{3,2},{4,5},{5,4},{6,7},{7,6},{8,9},{9,8},{10,11... | collective-permute-start | bytes 1572872 | tf_op jit(solution)/shard_map/ppermute | solution.py:249
  35.1 3.5 %collective-permute-start.4 = (bf16[128,1024]{1,0:T(8,128)(2,1)S(1)}, bf16[128,1024]{1,0:T(8,128)(2,1)S(1)}, u32[]{:S(2)}, u32[]{:S(2)}) collective-permute-start(bf16[128,1024]{1,0:T(8,128)(2,1)S(1)} %collective-permute-done.1.ring1_ref), channel_id=1, source_target_pairs={{0,2},{1,7},{2,4},{3,1},{4,6},{5,3},{6,0},{7,5},{8,10},{9,15},{10,... | collective-permute-start | bytes 786440 | tf_op jit(solution)/shard_map/ppermute | solution.py:246
  38.6 4.8 %collective-permute-done.4.first_ref = bf16[128,1024]{1,0:T(8,128)(2,1)S(1)} collective-permute-done((bf16[128,1024]{1,0:T(8,128)(2,1)S(1)}, bf16[128,1024]{1,0:T(8,128)(2,1)S(1)}, u32[]{:S(2)}, u32[]{:S(2)}) %collective-permute-start.4) | collective-permute-done | bytes 262176 | tf_op jit(solution)/shard_map/ppermute | solution.py:246
  43.4 4.0 %collective-permute-start.5 = (bf16[128,1024]{1,0:T(8,128)(2,1)S(1)}, bf16[128,1024]{1,0:T(8,128)(2,1)S(1)}, u32[]{:S(2)}, u32[]{:S(2)}) collective-permute-start(bf16[128,1024]{1,0:T(8,128)(2,1)S(1)} %collective-permute-done.4.first_ref), channel_id=1, source_target_pairs={{0,1},{1,0},{2,3},{3,2},{4,5},{5,4},{6,7},{7,6},{8,9},{9,8},{10,11... | collective-permute-start | bytes 786440 | tf_op jit(solution)/shard_map/ppermute | solution.py:249
  47.4 3.5 %shard_map.120.blocks_ref = bf16[8,512,1024]{2,1,0:T(8,128)(2,1)S(1)} custom-call(bf16[512,8192]{1,0:T(8,128)(2,1)} %weight_hbm.1), custom_call_target="tpu_custom_call" | custom-call | flops 1048576 | bytes 4194304 | tf_op jit(solution)/shard_map/pallas_call | solution.py:214
  50.9 0.8 shard_map.121.acc_ref
  51.8 0.0 copy-start.1
  51.8 0.8 shard_map.122.acc_ref
  52.6 0.0 copy-start.3
  52.6 0.0 copy-start.6
  52.7 0.8 shard_map.123.acc_ref
  53.5 2.2 %shard_map.124 = (bf16[128,512]{1,0:T(8,128)(2,1)S(1)}, bf16[128,512]{1,0:T(8,128)(2,1)}, f32[16,24,128]{2,1,0:T(8,128)S(1)}) custom-call(bf16[8,512,1024]{2,1,0:T(8,128)(2,1)S(1)} %shard_map.120.blocks_ref, bf16[128,1024]{1,0:T(8,128)(2,1)S(1)} %collective-permute-done.4.first_ref, bf16[128,1024]{1,0:T(8,128)(2,1)S(1)} %collective-permute-done.5.second_ref, ...), custom_call_target="tpu_custom_call" | custom-call | flops 536870912 | bytes 4194304 | tf_op jit(solution)/shard_map/pallas_call | solution.py:214
  55.7 30.1 %all_to_all.10.got_ref = f32[16,24,128]{2,1,0:T(8,128)S(1)} all-to-all(f32[16,24,128]{2,1,0:T(8,128)S(1)} %get-tuple-element.29), channel_id=1, replica_groups={{0,64,128,192,256,320,384,448,512,576,640,704,768,832,896,960},{8,72,13..., dimensions={0} | all-to-all | bytes 393216 | tf_op jit(solution)/shard_map/all_to_all | solution.py:232
  85.8 0.7 shard_map.126
  86.5 3.5 %all-to-all-start.1 = ((f32[16,24,128]{2,1,0:T(8,128)}), f32[16,24,128]{2,1,0:T(8,128)S(1)}, u32[]{:S(2)}, u32[]{:S(2)}) async-start(f32[16,24,128]{2,1,0:T(8,128)} %shard_map.126), calls=%async_computation.1 | async-start | bytes 393216 | tf_op jit(solution)/shard_map/all_to_all | solution.py:232
  90.0 1.3 %collective-permute-start.7 = (bf16[128,512]{1,0:T(8,128)(2,1)S(1)}, bf16[128,512]{1,0:T(8,128)(2,1)S(1)}, u32[]{:S(2)}, u32[]{:S(2)}) collective-permute-start(bf16[128,512]{1,0:T(8,128)(2,1)S(1)} %get-tuple-element.25.conv_ref), channel_id=1, source_target_pairs={{8,0},{16,8},{24,16},{32,24},{40,32},{48,40},{56,48},{64,56},{72,6... | collective-permute-start | bytes 393224 | tf_op jit(solution)/shard_map/ppermute | solution.py:228
  91.3 8.5 %collective-permute-done.7.after_ref = bf16[128,512]{1,0:T(8,128)(2,1)S(1)} collective-permute-done((bf16[128,512]{1,0:T(8,128)(2,1)S(1)}, bf16[128,512]{1,0:T(8,128)(2,1)S(1)}, u32[]{:S(2)}, u32[]{:S(2)}) %collective-permute-start.7) | collective-permute-done | bytes 131104 | tf_op jit(solution)/shard_map/ppermute | solution.py:228
  99.8 1.4 %shard_map.125 = (bf16[128,512]{1,0:T(8,128)(2,1)}, bf16[128,512]{1,0:T(8,128)(2,1)}) custom-call(bf16[128,512]{1,0:T(8,128)(2,1)S(1)} %get-tuple-element.25.conv_ref, bf16[128,512]{1,0:T(8,128)(2,1)S(1)} %collective-permute-done.7.after_ref, bf16[128,512]{1,0:T(8,128)(2,1)S(1)} %copy-done.3, bf16[128,512]{1,0:T(8,128)(2,1)S(1)} %copy-done.2, ...), custom_call_target="tpu_custom_call" | custom-call | flops 268435456 | bytes 4194304 | tf_op jit(solution)/shard_map/pallas_call | solution.py:214
  101.3 0.6 shard_map.127
  (14 shorter events, 0.0 us)
Async XLA Ops:
  0.6 18.0 %collective-permute-start.2 = (bf16[128,1024]{1,0:T(8,128)(2,1)}, bf16[128,1024]{1,0:T(8,128)(2,1)S(1)}, u32[]{:S(2)}, u32[]{:S(2)}) collective-permute-start(bf16[128,1024]{1,0:T(8,128)(2,1)} %own_ref.1), channel_id=1, source_target_pairs={{0,1},{1,0},{2,3},{3,2},{4,5},{5,4},{6,7},{7,6},{8,9},{9,8},{10,11... | collective-permute-start | bytes 786440 | tf_op jit(solution)/shard_map/ppermute | solution.py:249
  16.7 9.3 %collective-permute-start.1 = (bf16[128,1024]{1,0:T(8,128)(2,1)}, bf16[128,1024]{1,0:T(8,128)(2,1)S(1)}, u32[]{:S(2)}, u32[]{:S(2)}) collective-permute-start(bf16[128,1024]{1,0:T(8,128)(2,1)} %own_ref.1), channel_id=1, source_target_pairs={{0,2},{1,7},{2,4},{3,1},{4,6},{5,3},{6,0},{7,5},{8,10},{9,15},{10,... | collective-permute-start | bytes 786440 | tf_op jit(solution)/shard_map/ppermute | solution.py:246
  18.6 9.4 %collective-permute-start.3 = (bf16[128,1024]{1,0:T(8,128)(2,1)S(1)}, bf16[128,1024]{1,0:T(8,128)(2,1)S(1)}, u32[]{:S(2)}, u32[]{:S(2)}) collective-permute-start(bf16[128,1024]{1,0:T(8,128)(2,1)S(1)} %collective-permute-done.2.swap_ref), channel_id=1, source_target_pairs={{0,2},{1,7},{2,4},{3,1},{4,6},{5,3},{6,0},{7,5},{8,10},{9,15},{10,... | collective-permute-start | bytes 786440 | tf_op jit(solution)/shard_map/ppermute | solution.py:246
  21.5 4.4 %collective-permute-start = (bf16[128,512]{1,0:T(8,128)(2,1)S(1)}, bf16[128,512]{1,0:T(8,128)(2,1)S(1)}, u32[]{:S(2)}, u32[]{:S(2)}) collective-permute-start(bf16[128,512]{1,0:T(8,128)(2,1)S(1)} %multiply_convert_fusion.inner_ref), channel_id=1, source_target_pairs={{0,8},{8,16},{16,24},{24,32},{32,40},{40,48},{48,56},{56,64},{64,7... | collective-permute-start | bytes 393224 | tf_op jit(solution)/shard_map/ppermute | solution.py:228
  22.8 0.7 copy-start.7
  28.0 0.9 copy-start
  28.9 0.7 copy-start.5
  31.0 19.9 %copy-start.4 = (bf16[128,1024]{1,0:T(8,128)(2,1)S(1)}, bf16[128,1024]{1,0:T(8,128)(2,1)}, u32[]{:S(2)}) copy-start(bf16[128,1024]{1,0:T(8,128)(2,1)} %own_ref.1) | copy-start | bytes 786436
  31.0 21.7 %collective-permute-start.6 = (bf16[2,128,1024]{2,1,0:T(8,128)(2,1)S(1)}, bf16[2,128,1024]{2,1,0:T(8,128)(2,1)S(1)}, u32[]{:S(2)}, u32[]{:S(2)}) collective-permute-start(bf16[2,128,1024]{2,1,0:T(8,128)(2,1)S(1)} %get-tuple-element.21), channel_id=1, source_target_pairs={{0,1},{1,0},{2,3},{3,2},{4,5},{5,4},{6,7},{7,6},{8,9},{9,8},{10,11... | collective-permute-start | bytes 1572872 | tf_op jit(solution)/shard_map/ppermute | solution.py:249
  35.1 8.3 %collective-permute-start.4 = (bf16[128,1024]{1,0:T(8,128)(2,1)S(1)}, bf16[128,1024]{1,0:T(8,128)(2,1)S(1)}, u32[]{:S(2)}, u32[]{:S(2)}) collective-permute-start(bf16[128,1024]{1,0:T(8,128)(2,1)S(1)} %collective-permute-done.1.ring1_ref), channel_id=1, source_target_pairs={{0,2},{1,7},{2,4},{3,1},{4,6},{5,3},{6,0},{7,5},{8,10},{9,15},{10,... | collective-permute-start | bytes 786440 | tf_op jit(solution)/shard_map/ppermute | solution.py:246
  43.4 10.1 %collective-permute-start.5 = (bf16[128,1024]{1,0:T(8,128)(2,1)S(1)}, bf16[128,1024]{1,0:T(8,128)(2,1)S(1)}, u32[]{:S(2)}, u32[]{:S(2)}) collective-permute-start(bf16[128,1024]{1,0:T(8,128)(2,1)S(1)} %collective-permute-done.4.first_ref), channel_id=1, source_target_pairs={{0,1},{1,0},{2,3},{3,2},{4,5},{5,4},{6,7},{7,6},{8,9},{9,8},{10,11... | collective-permute-start | bytes 786440 | tf_op jit(solution)/shard_map/ppermute | solution.py:249
  51.8 1.7 %copy-start.1 = (bf16[128,512]{1,0:T(8,128)(2,1)S(1)}, bf16[128,512]{1,0:T(8,128)(2,1)}, u32[]{:S(2)}) copy-start(bf16[128,512]{1,0:T(8,128)(2,1)} %query_ref.3) | copy-start | bytes 393220
  52.6 47.2 %copy-start.2 = (bf16[128,512]{1,0:T(8,128)(2,1)S(1)}, bf16[128,512]{1,0:T(8,128)(2,1)}, u32[]{:S(2)}) copy-start(bf16[128,512]{1,0:T(8,128)(2,1)} %value_ref.1) | copy-start | bytes 393220
  52.6 47.2 %copy-start.3 = (bf16[128,512]{1,0:T(8,128)(2,1)S(1)}, bf16[128,512]{1,0:T(8,128)(2,1)}, u32[]{:S(2)}) copy-start(bf16[128,512]{1,0:T(8,128)(2,1)} %key_ref.1) | copy-start | bytes 393220
  52.6 47.2 %copy-start.6 = (f32[512]{0:T(512)S(1)}, f32[512]{0:T(512)}, u32[]{:S(2)}) copy-start(f32[512]{0:T(512)} %param.11) | copy-start | bytes 6148
  86.5 14.8 %all-to-all-start.1 = ((f32[16,24,128]{2,1,0:T(8,128)}), f32[16,24,128]{2,1,0:T(8,128)S(1)}, u32[]{:S(2)}, u32[]{:S(2)}) async-start(f32[16,24,128]{2,1,0:T(8,128)} %shard_map.126), calls=%async_computation.1 | async-start | bytes 393216 | tf_op jit(solution)/shard_map/all_to_all | solution.py:232
  90.0 9.8 %collective-permute-start.7 = (bf16[128,512]{1,0:T(8,128)(2,1)S(1)}, bf16[128,512]{1,0:T(8,128)(2,1)S(1)}, u32[]{:S(2)}, u32[]{:S(2)}) collective-permute-start(bf16[128,512]{1,0:T(8,128)(2,1)S(1)} %get-tuple-element.25.conv_ref), channel_id=1, source_target_pairs={{8,0},{16,8},{24,16},{32,24},{40,32},{48,40},{56,48},{64,56},{72,6... | collective-permute-start | bytes 393224 | tf_op jit(solution)/shard_map/ppermute | solution.py:228
